TPU v7x, 32 devices: a whole 2x2x4 slice. The times are simulated.
32 devices in a mesh: slab: 8 (over z, y), sub: 4 (over x, core).
Axes of the slice: x: 2, y: 2, z: 4, core: 2. Of those that a mesh axis runs over, the one named last changes fastest.
Arguments:
- start: float32 [64, 6, 2, 16, 128], P(('slab', 'sub')), may hold values from -20 to 20
- inv_factor: bfloat16 [1024, 2, 128, 128], P(('slab', 'sub')), as said below
- partner: int32 [64, 6], P(('slab', 'sub')), may hold values from -1 to 63, as said below
- partner_face: int32 [64, 6], P(('slab', 'sub')), may hold values from -1 to 5, as said below
- elem_class: int32 [64, 16], P(('slab', 'sub')), may hold values from 0 to 3
- elem_face: int32 [64, 16], P(('slab', 'sub')), may hold values from 0 to 5
- load_map: bfloat16 [4, 2, 128, 128], replicated, may hold values from -0.375 to 0.375
- trace_map: bfloat16 [4, 2, 128, 128], replicated, may hold values from -0.25 to 0.25
Outputs:
- last_block: float32 [64, 6, 2, 16, 128], P(('slab', 'sub'))
- hessenberg: float32 [4, 5, 16, 16], replicated
Inputs may be any that keep to these rules, and one draw needn't show every extreme that they name: Global subdomain s lies on device s // 2 of the joined axes. Across faces 0 and 1 the partner lies on the same device; across face 2 on the device one lower along sub, face 3 one higher along sub, face 4 one lower along slab, face 5 one higher along slab, and -1 exactly where no such device exists. `partner_face`: faces 0 and 1 meet face 0 or 1 of their partner; faces 2, 3, 4, 5 meet faces 3, 2, 5, 4; -1 exactly where partner is -1. `inv_factor`: each factor is lower triangular with a real diagonal of 0.5 to 2 and a small imaginary diagonal.
All inputs are finite; a program needn't handle non-finite values.
Results may differ from a plain program's by a relative error of at most 0.013.
Values sent between devices are 32-bit elements; how exact they have to be, the bound alone decides.
No kernel may reach another device: no remote copies, remote signals or barrier semaphores. Data moves between devices by JAX's collectives and lax.ppermute only.
A program may use at most 64 MiB of HBM per device.

v0:
```python
import jax
import jax.numpy as jnp
from jax import lax
from jax.sharding import PartitionSpec as P

ITERS = 4


HIGHEST_PRECISION = lax.Precision.HIGHEST


def extended(x, sides, width):
    for axis, dim in sides:
        count, length = (lax.axis_size(axis), x.shape[dim])
        up = [(i, (i + 1) % count) for i in range(count - 1)]
        down = [(j, i) for i, j in up]
        last = lax.slice_in_dim(x, length - width, length, axis=dim)
        leading = lax.slice_in_dim(x, 0, width, axis=dim)
        before = lax.ppermute(last, axis, up)
        after = lax.ppermute(leading, axis, down)
        x = jnp.concatenate([before, x, after], axis=dim)
    return x


def complex_apply(layout, matrix_real, matrix_imag, vec_real, vec_imag):
    real_part = jnp.einsum(
        layout, matrix_real, vec_real, preferred_element_type=jnp.float32
    ) - jnp.einsum(layout, matrix_imag, vec_imag, preferred_element_type=jnp.float32)
    imag_part = jnp.einsum(
        layout, matrix_real, vec_imag, preferred_element_type=jnp.float32
    ) + jnp.einsum(layout, matrix_imag, vec_real, preferred_element_type=jnp.float32)
    return (real_part, imag_part)


def factor_apply(inv_factor, vector_b, adjoint):
    factor_real = inv_factor[:, 0]
    factor_imag = inv_factor[:, 1]
    vec_real = vector_b[:, 0]
    vec_imag = vector_b[:, 1]
    if adjoint:
        layout = "eji,erj->eri"
        real_part = jnp.einsum(
            layout, factor_real, vec_real, preferred_element_type=jnp.float32
        ) + jnp.einsum(layout, factor_imag, vec_imag, preferred_element_type=jnp.float32)
        imag_part = jnp.einsum(
            layout, factor_real, vec_imag, preferred_element_type=jnp.float32
        ) - jnp.einsum(layout, factor_imag, vec_real, preferred_element_type=jnp.float32)
    else:
        layout = "eij,erj->eri"
        real_part, imag_part = complex_apply(layout, factor_real, factor_imag, vec_real, vec_imag)
    return jnp.stack([real_part, imag_part], axis=1)


def partner_traces(outgoing, partner, partner_face):
    sub_count = outgoing.shape[0]
    has_partner = partner >= 0
    local_index = jnp.where(has_partner, partner % sub_count, 0)
    face_index = jnp.where(has_partner, partner_face, 0)
    beside_all = extended(outgoing[None, None], (("slab", 0), ("sub", 1)), 1)
    trace_pool = beside_all.reshape((9 * sub_count * 6,) + outgoing.shape[2:])
    block_table = jnp.array([4, 4, 3, 5, 1, 7], jnp.int32)
    source_slot = (block_table[None, :] * sub_count + local_index) * 6 + face_index
    picked = trace_pool[source_slot]
    return jnp.where(has_partner[:, :, None, None, None], picked, 0.0)


def apply_operator(
    vector, inv_factor, partner, partner_face, elem_class, elem_face, load_map, trace_map
):
    sub_count = vector.shape[0]
    elem_count = elem_class.shape[1]
    rhs_count = vector.shape[3]
    wave_count = load_map.shape[2]
    vector_b = vector.astype(jnp.bfloat16)
    elem_load_map = load_map[elem_class]
    elem_trace_map = trace_map[elem_class]
    face_traces = jnp.take_along_axis(vector_b, elem_face[:, :, None, None, None], axis=1)
    load_real, load_imag = complex_apply(
        "sepq,serq->serp",
        elem_load_map[:, :, 0],
        elem_load_map[:, :, 1],
        face_traces[:, :, 0],
        face_traces[:, :, 1],
    )
    chosen_b = (
        jnp.stack([load_real, load_imag], axis=2)
        .astype(jnp.bfloat16)
        .reshape(sub_count * elem_count, 2, rhs_count, wave_count)
    )
    middle = factor_apply(inv_factor, chosen_b, False).astype(jnp.bfloat16)
    coefficients = (
        factor_apply(inv_factor, middle, True)
        .astype(jnp.bfloat16)
        .reshape(sub_count, elem_count, 2, rhs_count, wave_count)
    )
    trace_real, trace_imag = complex_apply(
        "seqp,serp->serq",
        elem_trace_map[:, :, 0],
        elem_trace_map[:, :, 1],
        coefficients[:, :, 0],
        coefficients[:, :, 1],
    )
    accumulated = jnp.stack([trace_real, trace_imag], axis=2)
    face_onehot = (elem_face[:, :, None] == jnp.arange(6, dtype=jnp.int32)[None, None, :]).astype(
        jnp.float32
    )
    outgoing = (
        jnp.einsum("sef,sexrq->sfxrq", face_onehot, accumulated, precision=HIGHEST_PRECISION)
        - vector
    )
    return vector - partner_traces(outgoing, partner, partner_face)


def local_inner(left, right):
    return jnp.einsum("sfxiq,sfxjq->ij", left, right, precision=HIGHEST_PRECISION)


def normalize(vector, gram_matrix):
    low_factor = jnp.linalg.cholesky(gram_matrix)
    identity = jnp.eye(gram_matrix.shape[0], dtype=jnp.float32)
    inverse = lax.linalg.triangular_solve(low_factor, identity, left_side=True, lower=True)
    return (
        jnp.einsum("sfxaq,ba->sfxbq", vector, inverse, precision=HIGHEST_PRECISION),
        low_factor.T,
    )


def body(start, inv_factor, partner, partner_face, elem_class, elem_face, load_map, trace_map):
    rhs_count = start.shape[3]
    entry_count = start.size // rhs_count * lax.axis_size("slab") * lax.axis_size("sub")
    start_gram = lax.psum(local_inner(start, start), ("slab", "sub")) / entry_count
    basis_block, upper_factor = normalize(start, start_gram)
    blocks = [basis_block]
    hessenberg = jnp.zeros((ITERS, ITERS + 1, rhs_count, rhs_count), jnp.float32)
    for number in range(ITERS):
        image_block = apply_operator(
            blocks[-1],
            inv_factor,
            partner,
            partner_face,
            elem_class,
            elem_face,
            load_map,
            trace_map,
        )
        stacked = jnp.stack(blocks)
        local_terms = jnp.einsum(
            "ksfxiq,sfxjq->kij", stacked, image_block, precision=HIGHEST_PRECISION
        )
        summed_terms, raw_gram = lax.psum(
            (local_terms, local_inner(image_block, image_block)), ("slab", "sub")
        )
        projection = summed_terms / entry_count
        image_block = image_block - jnp.einsum(
            "ksfxaq,kab->sfxbq", stacked, projection, precision=HIGHEST_PRECISION
        )
        gram_matrix = raw_gram / entry_count - jnp.einsum(
            "kai,kaj->ij", projection, projection, precision=HIGHEST_PRECISION
        )
        basis_block, upper_factor = normalize(image_block, gram_matrix)
        hessenberg = hessenberg.at[number, : number + 1].set(projection)
        hessenberg = hessenberg.at[number, number + 1].set(upper_factor)
        blocks.append(basis_block)
    return (blocks[-1], hessenberg)


def solution(mesh):
    placed = (
        P(("slab", "sub"), None, None, None, None),
        P(("slab", "sub"), None, None, None),
        P(("slab", "sub"), None),
        P(("slab", "sub"), None),
        P(("slab", "sub"), None),
        P(("slab", "sub"), None),
        P(),
        P(),
    )
    return jax.shard_map(
        body,
        mesh=mesh,
        in_specs=placed,
        out_specs=(P(("slab", "sub"), None, None, None, None), P()),
        check_vma=False,
    )
```

profile of v0, /device:TPU:0, one launch (start us, length us, event | category | flops | bytes accessed | tf_op | source)
XLA Modules:
  0.0 421.2 jit_solution(14362382191184048011)
XLA Ops:
  2.8 2.1 gather_fusion
  7.2 42.0 %psum.63 = f32[16,16]{0,1:T(8,128)S(1)} all-reduce(f32[16,16]{0,1:T(8,128)S(1)} %convolution_bitcast_fusion.21), channel_id=1, replica_groups=mesh['slab'=8,'sub'=4] {'slab','sub'}, use_global_device_ids=true, to_apply=%region_0.0 | all-reduce | flops 256 | bytes 2048 | tf_op jit(solution)/shard_map/psum | solution.py:131
  55.4 2.0 fusion.119
  65.1 2.1 gather_fusion.1
  73.9 4.8 %collective-permute-start = (f32[1,1,2,6,2,16,128]{6,5,4,3,2,1,0:T(8,128)S(1)}, f32[1,1,2,6,2,16,128]{6,5,4,3,2,1,0:T(8,128)S(1)}, u32[]{:S(2)}, u32[]{:S(2)}) collective-permute-start(f32[1,1,2,6,2,16,128]{6,5,4,3,2,1,0:T(8,128)S(1)} %fusion.108), channel_id=1, source_target_pairs={{0,4},{4,8},{8,12},{12,16},{16,20},{20,24},{24,28},{1,5},{5,9},{9,... | collective-permute-start | bytes 589832 | tf_op jit(solution)/shard_map/ppermute | solution.py:19
  80.4 3.9 collective-permute-done
  86.4 3.9 collective-permute-start.2
  91.4 2.7 pad_maximum_fusion
  94.2 2.0 gather_fusion.2
  97.0 48.7 %all-reduce.4 = (f32[16,16]{0,1:T(8,128)S(1)}, f32[1,16,16]{2,1,0:T(8,128)S(1)}) all-reduce(f32[16,16]{0,1:T(8,128)S(1)} %convolution_bitcast_fusion.20, f32[1,16,16]{2,1,0:T(8,128)S(1)} %convolution_bitcast_fusion.19), channel_id=1, replica_groups=mesh['slab'=8,'sub'=4] {'slab','sub'}, use_global_device_ids=true, to_apply=%region_3.7 | all-reduce | flops 512 | bytes 4096 | tf_op jit(solution)/shard_map/psum | solution.py:150
  166.4 4.8 %collective-permute-start.4 = (f32[1,1,2,6,2,16,128]{6,5,4,3,2,1,0:T(8,128)S(1)}, f32[1,1,2,6,2,16,128]{6,5,4,3,2,1,0:T(8,128)S(1)}, u32[]{:S(2)}, u32[]{:S(2)}) collective-permute-start(f32[1,1,2,6,2,16,128]{6,5,4,3,2,1,0:T(8,128)S(1)} %fusion.103), channel_id=1, source_target_pairs={{0,4},{4,8},{8,12},{12,16},{16,20},{20,24},{24,28},{1,5},{5,9},{9,... | collective-permute-start | bytes 589832 | tf_op jit(solution)/shard_map/ppermute | solution.py:19
  172.9 3.8 collective-permute-done.4
  178.1 3.1 collective-permute-start.6
  184.1 2.0 gather_fusion.3
  187.1 47.7 %all-reduce.3 = (f32[2,16,16]{2,1,0:T(8,128)S(1)}, f32[16,16]{0,1:T(8,128)S(1)}) all-reduce(f32[2,16,16]{2,1,0:T(8,128)S(1)} %convolution_bitcast_fusion.7, f32[16,16]{0,1:T(8,128)S(1)} %convolution_bitcast_fusion.18), channel_id=1, replica_groups=mesh['slab'=8,'sub'=4] {'slab','sub'}, use_global_device_ids=true, to_apply=%region_6.10 | all-reduce | flops 768 | bytes 6144 | tf_op jit(solution)/shard_map/psum | solution.py:150
  255.5 4.9 %collective-permute-start.8 = (f32[1,1,2,6,2,16,128]{6,5,4,3,2,1,0:T(8,128)S(1)}, f32[1,1,2,6,2,16,128]{6,5,4,3,2,1,0:T(8,128)S(1)}, u32[]{:S(2)}, u32[]{:S(2)}) collective-permute-start(f32[1,1,2,6,2,16,128]{6,5,4,3,2,1,0:T(8,128)S(1)} %fusion.101), channel_id=1, source_target_pairs={{0,4},{4,8},{8,12},{12,16},{16,20},{20,24},{24,28},{1,5},{5,9},{9,... | collective-permute-start | bytes 589832 | tf_op jit(solution)/shard_map/ppermute | solution.py:19
  262.0 4.0 collective-permute-done.8
  267.4 3.1 collective-permute-start.10
  273.4 2.0 gather_fusion.4
  276.6 48.9 %all-reduce.2 = (f32[3,16,16]{2,1,0:T(8,128)S(1)}, f32[16,16]{0,1:T(8,128)S(1)}) all-reduce(f32[3,16,16]{2,1,0:T(8,128)S(1)} %convolution_bitcast_fusion.6, f32[16,16]{0,1:T(8,128)S(1)} %convolution_bitcast_fusion.17), channel_id=1, replica_groups=mesh['slab'=8,'sub'=4] {'slab','sub'}, use_global_device_ids=true, to_apply=%region_8.12 | all-reduce | flops 1024 | bytes 8192 | tf_op jit(solution)/shard_map/psum | solution.py:150
  346.3 4.8 %collective-permute-start.12 = (f32[1,1,2,6,2,16,128]{6,5,4,3,2,1,0:T(8,128)S(1)}, f32[1,1,2,6,2,16,128]{6,5,4,3,2,1,0:T(8,128)S(1)}, u32[]{:S(2)}, u32[]{:S(2)}) collective-permute-start(f32[1,1,2,6,2,16,128]{6,5,4,3,2,1,0:T(8,128)S(1)} %fusion.99), channel_id=1, source_target_pairs={{0,4},{4,8},{8,12},{12,16},{16,20},{20,24},{24,28},{1,5},{5,9},{9,... | collective-permute-start | bytes 589832 | tf_op jit(solution)/shard_map/ppermute | solution.py:19
  352.8 3.7 collective-permute-done.12
  357.9 3.8 collective-permute-start.14
  366.6 47.3 %all-reduce.1 = (f32[4,16,16]{2,1,0:T(8,128)S(1)}, f32[16,16]{0,1:T(8,128)S(1)}) all-reduce(f32[4,16,16]{2,1,0:T(8,128)S(1)} %convolution_bitcast_fusion.5, f32[16,16]{0,1:T(8,128)S(1)} %convolution_bitcast_fusion.16), channel_id=1, replica_groups=mesh['slab'=8,'sub'=4] {'slab','sub'}, use_global_device_ids=true, to_apply=%region_10.14 | all-reduce | flops 1280 | bytes 10240 | tf_op jit(solution)/shard_map/psum | solution.py:150
  (259 shorter events, 121.5 us)
Async XLA Ops:
  6.9 47.9 %copy-start.2 = (bf16[32,2,128,128]{3,2,0,1:T(8,128)(2,1)}, bf16[32,2,128,128]{3,2,0,1:T(8,128)(2,1)S(1)}, u32[]{:S(2)}) copy-start(bf16[32,2,128,128]{3,2,0,1:T(8,128)(2,1)S(1)} %copy.19) | copy-start | bytes 6291460
  72.0 18.3 %copy-start.24 = (s32[2,6]{1,0:T(2,128)S(1)}, s32[2,6]{1,0:T(2,128)}, u32[]{:S(2)}) copy-start(s32[2,6]{1,0:T(2,128)} %param.36) | copy-start | bytes 148
  72.0 18.3 %copy-start.25 = (s32[2,6]{1,0:T(2,128)S(1)}, s32[2,6]{1,0:T(2,128)}, u32[]{:S(2)}) copy-start(s32[2,6]{1,0:T(2,128)} %param.35) | copy-start | bytes 148
  72.0 18.3 %copy-start.26 = (s32[6]{0:T(128)S(1)}, s32[6]{0:T(128)}, u32[]{:S(2)}) copy-start(s32[6]{0:T(128)} %constant.343) | copy-start | bytes 76
  72.6 7.8 %collective-permute-start.1 = (f32[1,1,2,6,2,16,128]{6,5,4,3,2,1,0:T(8,128)S(1)}, f32[1,1,2,6,2,16,128]{6,5,4,3,2,1,0:T(8,128)S(1)}, u32[]{:S(2)}, u32[]{:S(2)}) collective-permute-start(f32[1,1,2,6,2,16,128]{6,5,4,3,2,1,0:T(8,128)S(1)} %fusion.108), channel_id=1, source_target_pairs={{4,0},{8,4},{12,8},{16,12},{20,16},{24,20},{28,24},{5,1},{9,5},{13... | collective-permute-start | bytes 589832 | tf_op jit(solution)/shard_map/ppermute | solution.py:20
  73.9 10.4 %collective-permute-start = (f32[1,1,2,6,2,16,128]{6,5,4,3,2,1,0:T(8,128)S(1)}, f32[1,1,2,6,2,16,128]{6,5,4,3,2,1,0:T(8,128)S(1)}, u32[]{:S(2)}, u32[]{:S(2)}) collective-permute-start(f32[1,1,2,6,2,16,128]{6,5,4,3,2,1,0:T(8,128)S(1)} %fusion.108), channel_id=1, source_target_pairs={{0,4},{4,8},{8,12},{12,16},{16,20},{20,24},{24,28},{1,5},{5,9},{9,... | collective-permute-start | bytes 589832 | tf_op jit(solution)/shard_map/ppermute | solution.py:19
  85.2 5.3 %collective-permute-start.3 = (f32[3,1,2,6,2,16,128]{6,5,4,3,2,1,0:T(8,128)}, f32[3,1,2,6,2,16,128]{6,5,4,3,2,1,0:T(8,128)}, u32[]{:S(2)}, u32[]{:S(2)}) collective-permute-start(f32[3,1,2,6,2,16,128]{6,5,4,3,2,1,0:T(8,128)} %pad_maximum_fusion.5), channel_id=1, source_target_pairs={{1,0},{2,1},{3,2},{5,4},{6,5},{7,6},{9,8},{10,9},{11,10},{13,12},{... | collective-permute-start | bytes 1769480 | tf_op jit(solution)/shard_map/ppermute | solution.py:20
  86.4 5.0 %collective-permute-start.2 = (f32[3,1,2,6,2,16,128]{6,5,4,3,2,1,0:T(8,128)}, f32[3,1,2,6,2,16,128]{6,5,4,3,2,1,0:T(8,128)}, u32[]{:S(2)}, u32[]{:S(2)}) collective-permute-start(f32[3,1,2,6,2,16,128]{6,5,4,3,2,1,0:T(8,128)} %pad_maximum_fusion.5), channel_id=1, source_target_pairs={{0,1},{1,2},{2,3},{4,5},{5,6},{6,7},{8,9},{9,10},{10,11},{12,13},{... | collective-permute-start | bytes 1769480 | tf_op jit(solution)/shard_map/ppermute | solution.py:19
  90.4 185.0 %copy-start.22 = (pred[2,6]{1,0:T(4,128)(4,1)}, pred[2,6]{1,0:T(4,128)(4,1)S(1)}, u32[]{:S(2)}) copy-start(pred[2,6]{1,0:T(4,128)(4,1)S(1)} %broadcast_compare_fusion) | copy-start | bytes 40
  165.1 7.9 %collective-permute-start.5 = (f32[1,1,2,6,2,16,128]{6,5,4,3,2,1,0:T(8,128)S(1)}, f32[1,1,2,6,2,16,128]{6,5,4,3,2,1,0:T(8,128)S(1)}, u32[]{:S(2)}, u32[]{:S(2)}) collective-permute-start(f32[1,1,2,6,2,16,128]{6,5,4,3,2,1,0:T(8,128)S(1)} %fusion.103), channel_id=1, source_target_pairs={{4,0},{8,4},{12,8},{16,12},{20,16},{24,20},{28,24},{5,1},{9,5},{13... | collective-permute-start | bytes 589832 | tf_op jit(solution)/shard_map/ppermute | solution.py:20
  166.4 10.4 %collective-permute-start.4 = (f32[1,1,2,6,2,16,128]{6,5,4,3,2,1,0:T(8,128)S(1)}, f32[1,1,2,6,2,16,128]{6,5,4,3,2,1,0:T(8,128)S(1)}, u32[]{:S(2)}, u32[]{:S(2)}) collective-permute-start(f32[1,1,2,6,2,16,128]{6,5,4,3,2,1,0:T(8,128)S(1)} %fusion.103), channel_id=1, source_target_pairs={{0,4},{4,8},{8,12},{12,16},{16,20},{20,24},{24,28},{1,5},{5,9},{9,... | collective-permute-start | bytes 589832 | tf_op jit(solution)/shard_map/ppermute | solution.py:19
  176.8 4.4 %collective-permute-start.7 = (f32[3,1,2,6,2,16,128]{6,5,4,3,2,1,0:T(8,128)S(1)}, f32[3,1,2,6,2,16,128]{6,5,4,3,2,1,0:T(8,128)S(1)}, u32[]{:S(2)}, u32[]{:S(2)}) collective-permute-start(f32[3,1,2,6,2,16,128]{6,5,4,3,2,1,0:T(8,128)S(1)} %pad_maximum_fusion.6), channel_id=1, source_target_pairs={{1,0},{2,1},{3,2},{5,4},{6,5},{7,6},{9,8},{10,9},{11,10},{13,12},{... | collective-permute-start | bytes 1769480 | tf_op jit(solution)/shard_map/ppermute | solution.py:20
  178.1 4.7 %collective-permute-start.6 = (f32[3,1,2,6,2,16,128]{6,5,4,3,2,1,0:T(8,128)S(1)}, f32[3,1,2,6,2,16,128]{6,5,4,3,2,1,0:T(8,128)S(1)}, u32[]{:S(2)}, u32[]{:S(2)}) collective-permute-start(f32[3,1,2,6,2,16,128]{6,5,4,3,2,1,0:T(8,128)S(1)} %pad_maximum_fusion.6), channel_id=1, source_target_pairs={{0,1},{1,2},{2,3},{4,5},{5,6},{6,7},{8,9},{9,10},{10,11},{12,13},{... | collective-permute-start | bytes 1769480 | tf_op jit(solution)/shard_map/ppermute | solution.py:19
  254.2 7.9 %collective-permute-start.9 = (f32[1,1,2,6,2,16,128]{6,5,4,3,2,1,0:T(8,128)S(1)}, f32[1,1,2,6,2,16,128]{6,5,4,3,2,1,0:T(8,128)S(1)}, u32[]{:S(2)}, u32[]{:S(2)}) collective-permute-start(f32[1,1,2,6,2,16,128]{6,5,4,3,2,1,0:T(8,128)S(1)} %fusion.101), channel_id=1, source_target_pairs={{4,0},{8,4},{12,8},{16,12},{20,16},{24,20},{28,24},{5,1},{9,5},{13... | collective-permute-start | bytes 589832 | tf_op jit(solution)/shard_map/ppermute | solution.py:20
  255.5 10.5 %collective-permute-start.8 = (f32[1,1,2,6,2,16,128]{6,5,4,3,2,1,0:T(8,128)S(1)}, f32[1,1,2,6,2,16,128]{6,5,4,3,2,1,0:T(8,128)S(1)}, u32[]{:S(2)}, u32[]{:S(2)}) collective-permute-start(f32[1,1,2,6,2,16,128]{6,5,4,3,2,1,0:T(8,128)S(1)} %fusion.101), channel_id=1, source_target_pairs={{0,4},{4,8},{8,12},{12,16},{16,20},{20,24},{24,28},{1,5},{5,9},{9,... | collective-permute-start | bytes 589832 | tf_op jit(solution)/shard_map/ppermute | solution.py:19
  266.1 5.0 %collective-permute-start.11 = (f32[3,1,2,6,2,16,128]{6,5,4,3,2,1,0:T(8,128)S(1)}, f32[3,1,2,6,2,16,128]{6,5,4,3,2,1,0:T(8,128)S(1)}, u32[]{:S(2)}, u32[]{:S(2)}) collective-permute-start(f32[3,1,2,6,2,16,128]{6,5,4,3,2,1,0:T(8,128)S(1)} %pad_maximum_fusion.7), channel_id=1, source_target_pairs={{1,0},{2,1},{3,2},{5,4},{6,5},{7,6},{9,8},{10,9},{11,10},{13,12},{... | collective-permute-start | bytes 1769480 | tf_op jit(solution)/shard_map/ppermute | solution.py:20
  267.4 4.7 %collective-permute-start.10 = (f32[3,1,2,6,2,16,128]{6,5,4,3,2,1,0:T(8,128)S(1)}, f32[3,1,2,6,2,16,128]{6,5,4,3,2,1,0:T(8,128)S(1)}, u32[]{:S(2)}, u32[]{:S(2)}) collective-permute-start(f32[3,1,2,6,2,16,128]{6,5,4,3,2,1,0:T(8,128)S(1)} %pad_maximum_fusion.7), channel_id=1, source_target_pairs={{0,1},{1,2},{2,3},{4,5},{5,6},{6,7},{8,9},{9,10},{10,11},{12,13},{... | collective-permute-start | bytes 1769480 | tf_op jit(solution)/shard_map/ppermute | solution.py:19
  344.4 17.3 %copy-start.17 = (f32[2,16,16]{2,1,0:T(8,128)S(1)}, f32[2,16,16]{2,1,0:T(8,128)}, u32[]{:S(2)}) copy-start(f32[2,16,16]{2,1,0:T(8,128)} %copy-done.16) | copy-start | bytes 6148
  344.4 17.3 %copy-start.20 = (f32[1,1,16,16]{2,3,1,0:T(8,128)S(1)}, f32[1,1,16,16]{2,3,1,0:T(8,128)}, u32[]{:S(2)}) copy-start(f32[1,1,16,16]{2,3,1,0:T(8,128)} %get-tuple-element.111) | copy-start | bytes 3076
  344.4 17.4 %copy-start.15 = (f32[3,16,16]{2,1,0:T(8,128)S(1)}, f32[3,16,16]{2,1,0:T(8,128)}, u32[]{:S(2)}) copy-start(f32[3,16,16]{2,1,0:T(8,128)} %copy-done.14) | copy-start | bytes 9220
  345.0 7.8 %collective-permute-start.13 = (f32[1,1,2,6,2,16,128]{6,5,4,3,2,1,0:T(8,128)S(1)}, f32[1,1,2,6,2,16,128]{6,5,4,3,2,1,0:T(8,128)S(1)}, u32[]{:S(2)}, u32[]{:S(2)}) collective-permute-start(f32[1,1,2,6,2,16,128]{6,5,4,3,2,1,0:T(8,128)S(1)} %fusion.99), channel_id=1, source_target_pairs={{4,0},{8,4},{12,8},{16,12},{20,16},{24,20},{28,24},{5,1},{9,5},{13... | collective-permute-start | bytes 589832 | tf_op jit(solution)/shard_map/ppermute | solution.py:20
  346.3 10.3 %collective-permute-start.12 = (f32[1,1,2,6,2,16,128]{6,5,4,3,2,1,0:T(8,128)S(1)}, f32[1,1,2,6,2,16,128]{6,5,4,3,2,1,0:T(8,128)S(1)}, u32[]{:S(2)}, u32[]{:S(2)}) collective-permute-start(f32[1,1,2,6,2,16,128]{6,5,4,3,2,1,0:T(8,128)S(1)} %fusion.99), channel_id=1, source_target_pairs={{0,4},{4,8},{8,12},{12,16},{16,20},{20,24},{24,28},{1,5},{5,9},{9,... | collective-permute-start | bytes 589832 | tf_op jit(solution)/shard_map/ppermute | solution.py:19
  356.6 5.3 %collective-permute-start.15 = (f32[3,1,2,6,2,16,128]{6,5,4,3,2,1,0:T(8,128)S(1)}, f32[3,1,2,6,2,16,128]{6,5,4,3,2,1,0:T(8,128)S(1)}, u32[]{:S(2)}, u32[]{:S(2)}) collective-permute-start(f32[3,1,2,6,2,16,128]{6,5,4,3,2,1,0:T(8,128)S(1)} %pad_maximum_fusion.9), channel_id=1, source_target_pairs={{1,0},{2,1},{3,2},{5,4},{6,5},{7,6},{9,8},{10,9},{11,10},{13,12},{... | collective-permute-start | bytes 1769480 | tf_op jit(solution)/shard_map/ppermute | solution.py:20
  357.9 5.4 %collective-permute-start.14 = (f32[3,1,2,6,2,16,128]{6,5,4,3,2,1,0:T(8,128)S(1)}, f32[3,1,2,6,2,16,128]{6,5,4,3,2,1,0:T(8,128)}, u32[]{:S(2)}, u32[]{:S(2)}) collective-permute-start(f32[3,1,2,6,2,16,128]{6,5,4,3,2,1,0:T(8,128)S(1)} %pad_maximum_fusion.9), channel_id=1, source_target_pairs={{0,1},{1,2},{2,3},{4,5},{5,6},{6,7},{8,9},{9,10},{10,11},{12,13},{... | collective-permute-start | bytes 1769480 | tf_op jit(solution)/shard_map/ppermute | solution.py:19
  (19 other events, 68.9 us)
where the time goes:
time: 423 us; the launch traced here: 421 us
  blocking collectives  235 us (56%)
  matrix products  61.2 us (14%)
  starting transfers between devices  43.5 us (10%)
  other arithmetic  33.8 us (8%)
  waiting for transfers between devices  24.3 us (6%)
  local copies, waits for them, and re-layouts  22.5 us (5%)
    psum x4, blocking collectives, body(): lax.psum((local_terms, local_inner(image_block, image_block)), ('slab', '...  193 us
    psum x1, blocking collectives, body(): lax.psum(local_inner(start, start), ('slab', 'sub')) / entry_count  42 us
    ppermute x8, starting transfers between devices, extended(): before = lax.ppermute(last, axis, up)  33.2 us
    ppermute x8, waiting for transfers between devices, extended(): before = lax.ppermute(last, axis, up)  18.9 us
    dot_general x12, matrix products, complex_apply(): jnp.einsum(layout, matrix_real, vec_real, preferred_element_type=jnp.floa...  12.9 us
    dot_general x12, matrix products, complex_apply(): jnp.einsum(layout, matrix_real, vec_imag, preferred_element_type=jnp.floa...  11.8 us
    another operation x15, other arithmetic, normalize(): low_factor = jnp.linalg.cholesky(gram_matrix)  10.7 us
    ppermute x8, starting transfers between devices, extended(): after = lax.ppermute(leading, axis, down)  10.3 us
  transfers between devices with their start and end apart: 16, of which 11 were waited for; matrix products, arithmetic and copies ran while one was open for 1% of the time, Pallas kernels for 0%

commit v1 on v0

v1 whole, which is shorter than its diff:
```python
import functools

import jax
import jax.numpy as jnp
from jax import lax
from jax.experimental import pallas as pl
from jax.experimental.pallas import tpu as pltpu
from jax.sharding import PartitionSpec as P

ITERS = 4
STEP_SCALE = 2.0**-8
KEPT = (0, 1, 3, 5)
GROUP = 4

F32 = jnp.float32
BF16 = jnp.bfloat16
HIGHEST = lax.Precision.HIGHEST


def dot(a, b, transposed=False, precision=None):
    dims = (((1,), (1 if transposed else 0,)), ((), ()))
    return lax.dot_general(a, b, dims, precision=precision, preferred_element_type=F32)


def two_parts(x):
    high = x.astype(BF16)
    return high, (x - high.astype(F32)).astype(BF16)


def doubled(x):
    return jnp.concatenate(two_parts(x), axis=0)


def compose(faces, slot_of, face_ref, class_ref, inv_ref, load_ref, trace_ref, add_to, scratch):
    first_ref, last_ref, held, sems, ids, part = scratch
    subs, elems = face_ref.shape
    half = load_ref.shape[2]

    def chosen(face):
        hit = face == faces[0]
        for f in faces[1:]:
            hit = hit | (face == f)
        return hit

    def fetch(e, count):
        hit = chosen(face_ref[e // elems, e % elems])

        @pl.when(hit)
        def _():
            ids[count] = e
            pltpu.make_async_copy(inv_ref.at[e], held.at[count], sems.at[count]).start()

        return count + hit.astype(jnp.int32)

    total = lax.fori_loop(0, subs * elems, fetch, jnp.int32(0))

    for c in range(load_ref.shape[0]):
        for x in range(2):
            first_ref[c, :, x * half : (x + 1) * half] = load_ref[c, x].astype(F32).T.astype(BF16)
        last_ref[c, :half, :half] = trace_ref[c, 0]
        last_ref[c, :half, half:] = -trace_ref[c, 1]
        last_ref[c, half:, :half] = trace_ref[c, 1]
        last_ref[c, half:, half:] = trace_ref[c, 0]

    def group(g, carry):
        for u in range(GROUP):
            at = g * GROUP + u

            @pl.when(at < total)
            def _():
                pltpu.make_async_copy(inv_ref.at[0], held.at[at], sems.at[at]).wait()

        places = []
        for u in range(GROUP):
            at = jnp.minimum(g * GROUP + u, total - 1)
            e = ids[at]
            face = face_ref[e // elems, e % elems]
            kind = class_ref[e // elems, e % elems]
            real = held[at, 0]
            imag = held[at, 1]
            wide = jnp.concatenate(
                [
                    jnp.concatenate([real, -imag], axis=1),
                    jnp.concatenate([imag, real], axis=1),
                ],
                axis=0,
            )
            out = dot(first_ref[kind], wide, True)
            out = dot(doubled(out), wide)
            out = dot(doubled(out[:half] + out[half:]), last_ref[kind], True)
            part[u] = out[:half] + out[half:]
            places.append((e // elems, face))
        for u in range(GROUP):
            add_to(places[u][0], places[u][1], jnp.where(g * GROUP + u < total, part[u], 0.0))
        return carry

    lax.fori_loop(0, (total + GROUP - 1) // GROUP, group, 0)


def compose_sent(face_ref, class_ref, partner_ref, inv_ref, load_ref, trace_ref, start_ref,
                 sub_ref, slab_ref, sum_ref, *scratch):
    subs = face_ref.shape[0]
    half = load_ref.shape[2]
    rhs = start_ref.shape[3]
    sum_ref[...] = jnp.zeros_like(sum_ref)

    def add_to(s, face, value):
        at = s * 2 + (face == 4).astype(jnp.int32)
        sum_ref[at] = sum_ref[at] + value

    compose((2, 4), None, face_ref, class_ref, inv_ref, load_ref, trace_ref, add_to, scratch)
    for out_ref, face in ((sub_ref, 2), (slab_ref, 4)):
        for s in range(subs):
            out_ref[s, :half] = sum_ref[s * 2 + (face == 4)]
            out_ref[s, half : half + rhs, :half] = start_ref[s, face, 0]
            out_ref[s, half : half + rhs, half:] = start_ref[s, face, 1]
            partner = partner_ref[s, face]
            there = (partner >= 0).astype(F32)
            local = jnp.where(partner >= 0, partner % subs, 0).astype(F32)
            out_ref[s, half + rhs : half + rhs + 8] = jnp.full((8, 2 * half), local, F32)
            out_ref[s, half + rhs + 8 : half + rhs + 16] = jnp.full((8, 2 * half), there, F32)


def spread(rows):
    half = rows.shape[0]
    lower = jnp.concatenate([-rows[:, half:], rows[:, :half]], axis=1)
    return two_parts(jnp.concatenate([rows, lower], axis=0))


def compose_kept(face_ref, class_ref, inv_ref, load_ref, trace_ref, high_ref, low_ref, sum_ref, *scratch):
    sum_ref[...] = jnp.zeros_like(sum_ref)

    def add_to(s, face, value):
        place = jnp.where(face == 3, 2, jnp.where(face == 5, 3, face))
        at = s * len(KEPT) + place
        sum_ref[at] = sum_ref[at] + value

    compose(KEPT, None, face_ref, class_ref, inv_ref, load_ref, trace_ref, add_to, scratch)
    for at in range(sum_ref.shape[0]):
        high, low = spread(sum_ref[at])
        high_ref[at] = high
        low_ref[at] = low


def krylov(partner_ref, partner_face_ref, high_ref, low_ref, from_sub_ref, from_slab_ref, start_ref,
           gram_ref, kept_ref, to_sub_ref, to_slab_ref, remote_high, remote_low, remote, out_ref):
    subs, _, _, rhs, half = start_ref.shape
    kept = len(KEPT)
    own = subs * kept
    sources = (from_sub_ref, from_slab_ref)

    for d in range(2):
        for t in range(subs):
            high, low = spread(sources[d][t, :half])
            remote_high[d * subs + t] = high
            remote_low[d * subs + t] = low
            remote[d * subs + t, :rhs] = sources[d][t, half : half + rhs]
    for s in range(subs):
        for i, face in enumerate(KEPT):
            kept_ref[s * kept + i, :rhs, :half] = start_ref[s, face, 0]
            kept_ref[s * kept + i, :rhs, half:] = start_ref[s, face, 1]

    def leaving(x, high, low):
        top, rest = two_parts(x)
        both = dot(jnp.concatenate([top, rest], axis=0), high)
        return both[:rhs] + both[rhs:] + dot(top, low) - x

    for k in range(ITERS):
        now = slice(k * rhs, (k + 1) * rhs)
        later = slice((k + 1) * rhs, (k + 2) * rhs)
        for at in range(own):
            out_ref[at] = leaving(kept_ref[at, now], high_ref[at], low_ref[at]) * STEP_SCALE
        for at in range(2 * subs):
            out_ref[own + at] = (
                leaving(remote[at, now], remote_high[at], remote_low[at]) * STEP_SCALE
            )
        for s in range(subs):
            for i, face in enumerate(KEPT):
                partner = partner_ref[s, face]
                local = partner % subs
                if i < 2:
                    local = local * 2 + partner_face_ref[s, face]
                    places = [p * kept + f for p in range(subs) for f in range(2)]
                else:
                    places = [own + (i - 2) * subs + p for p in range(subs)]
                value = out_ref[places[0]]
                for p in range(1, len(places)):
                    value = jnp.where(local == p, out_ref[places[p]], value)
                kept_ref[s * kept + i, later] = jnp.where(partner >= 0, value, 0.0)
        for d in range(2):
            for t in range(subs):
                local = sources[d][t, half + rhs : half + rhs + 1]
                there = sources[d][t, half + rhs + 8 : half + rhs + 9]
                value = out_ref[2 + d]
                for s in range(1, subs):
                    value = jnp.where(local > s - 0.5, out_ref[s * kept + 2 + d], value)
                remote[d * subs + t, later] = jnp.where(there > 0.5, value, 0.0)

    total = None
    for at in range(own + 2 * subs):
        rows = kept_ref[at] if at < own else remote[at - own]
        term = dot(rows, rows, True, HIGHEST)
        total = term if total is None else total + term
    first = total[:rhs, :rhs]
    for face in (2, 4):
        for s in range(subs):
            alone = jnp.where(partner_ref[s, face] < 0, 1.0, 0.0)
            for x in range(2):
                rows = start_ref[s, face, x] * alone
                first = first + dot(rows, rows, True, HIGHEST)
    for d, to_ref in enumerate((to_sub_ref, to_slab_ref)):
        for t in range(subs):
            to_ref[t] = remote[d * subs + t, rhs:]

    gram_ref[...] = jnp.zeros_like(gram_ref)
    for row, (blocks) in enumerate(((4, 1, 0), (3, 2))):
        lane = 0
        for i in blocks:
            width = (i + 1) * rhs
            piece = first if i == 0 else total[i * rhs : (i + 1) * rhs, :width]
            gram_ref[row * rhs : (row + 1) * rhs, lane : lane + width] = piece
            lane += width


def finish(count, gram_ref, kept_ref, back_sub_ref, back_slab_ref, start_ref, last_ref, hess_ref,
           upper_ref, inverse_ref):
    subs, _, _, rhs, half = start_ref.shape
    kept = len(KEPT)
    size = (ITERS + 1) * rhs
    lanes = 128
    offset = {}
    for row, (blocks) in enumerate(((4, 1, 0), (3, 2))):
        lane = 0
        for i in blocks:
            offset[i] = (row, lane)
            lane += (i + 1) * rhs
    upper_ref[...] = jnp.zeros_like(upper_ref)
    for i in range(ITERS + 1):
        row, lane = offset[i]
        width = (i + 1) * rhs
        upper_ref[i * rhs : (i + 1) * rhs, :width] = (
            gram_ref[row * rhs : (row + 1) * rhs, lane : lane + width] / count
        )
    lower = upper_ref[...]
    down = lax.broadcasted_iota(jnp.int32, (lanes, lanes), 0)
    across = lax.broadcasted_iota(jnp.int32, (lanes, lanes), 1)
    square = jnp.where(down >= across, lower, 0.0)
    full = jnp.where(down >= across, lower, square.T)

    blocks = size // 8
    work = [full[8 * i : 8 * i + 8] for i in range(blocks)]
    side = [
        (down[8 * i : 8 * i + 8] == across[8 * i : 8 * i + 8]).astype(F32) for i in range(blocks)
    ]
    sub_row = lax.broadcasted_iota(jnp.int32, (8, lanes), 0)
    for j in range(size):
        i, r = divmod(j, 8)
        row = jnp.broadcast_to(work[i][r : r + 1], (8, lanes))
        other = jnp.broadcast_to(side[i][r : r + 1], (8, lanes))
        pivot = jnp.broadcast_to(row[:, j : j + 1], (8, lanes))
        root = lax.rsqrt(pivot)
        scaled = row * root
        other = other * root
        upper_ref[j : j + 1, :] = scaled[:1]
        inverse_ref[j : j + 1, :] = other[:1]
        for m in range(i, blocks):
            if 8 * m + 7 <= j:
                continue
            column = jnp.broadcast_to(work[m][:, j : j + 1], (8, lanes)) * root
            if m == i:
                column = jnp.where(sub_row > r, column, 0.0)
            work[m] = work[m] - column * scaled
            side[m] = side[m] - column * other
    upper_ref[size:, :] = jnp.zeros((lanes - size, lanes), F32)
    inverse_ref[size:, :] = jnp.zeros((lanes - size, lanes), F32)

    upper = jnp.where(down <= across, upper_ref[...], 0.0)
    inverse = jnp.where(down >= across, inverse_ref[...], 0.0)
    shifted = jnp.concatenate([upper[:, rhs:], jnp.zeros((lanes, rhs), F32)], axis=1)
    moved = dot(shifted, inverse, True, HIGHEST) * (1.0 / STEP_SCALE)
    unit = (down[:rhs, :rhs] == across[:rhs, :rhs]).astype(F32)
    for k in range(ITERS):
        for j in range(ITERS + 1):
            if j > k + 1:
                hess_ref[k, j] = jnp.zeros((rhs, rhs), F32)
                continue
            block = moved[j * rhs : (j + 1) * rhs, k * rhs : (k + 1) * rhs]
            block = block if (j + k) % 2 else -block
            hess_ref[k, j] = block + unit if j == k else block

    mix = inverse[ITERS * rhs : size, :size]
    for s in range(subs):
        for i, face in enumerate(KEPT):
            value = dot(mix, kept_ref[s * kept + i], False, HIGHEST)
            last_ref[s, face, 0] = value[:, :half]
            last_ref[s, face, 1] = value[:, half:]
        for face, back_ref in ((2, back_sub_ref), (4, back_slab_ref)):
            first = jnp.concatenate([start_ref[s, face, 0], start_ref[s, face, 1]], axis=1)
            rows = jnp.concatenate([first, back_ref[s]], axis=0)
            value = dot(mix, rows, False, HIGHEST)
            last_ref[s, face, 0] = value[:, :half]
            last_ref[s, face, 1] = value[:, half:]


def summed(x, axes):
    for axis in axes:
        count, stride = lax.axis_size(axis), 1
        while stride < count:
            rest = count // stride
            ways = next(p for p in range(2, rest + 1) if rest % p == 0)
            received = []
            for d in range(1, ways):
                pairs = []
                for i in range(count):
                    digit = (i // stride) % ways
                    pairs.append((i, i + ((digit + d) % ways - digit) * stride))
                received.append(lax.ppermute(x, axis, pairs))
            for y in received:
                x = x + y
            stride *= ways
    return x


def body(start, inv_factor, partner, partner_face, elem_class, elem_face, load_map, trace_map):
    subs, _, _, rhs, half = start.shape
    elems = elem_class.shape[1]
    classes = load_map.shape[0]
    kept = len(KEPT)
    count = start.size // rhs * lax.axis_size("slab") * lax.axis_size("sub")
    smem = pl.BlockSpec(memory_space=pltpu.SMEM)
    vmem = pl.BlockSpec(memory_space=pltpu.VMEM)
    hbm = pl.BlockSpec(memory_space=pl.ANY)

    def scratch(sums):
        return [
            pltpu.VMEM((sums, half, 2 * half), F32),
            pltpu.VMEM((classes, half, 2 * half), BF16),
            pltpu.VMEM((classes, 2 * half, 2 * half), BF16),
            pltpu.VMEM((subs * elems, 2, half, half), BF16),
            pltpu.SemaphoreType.DMA((subs * elems,)),
            pltpu.SMEM((subs * elems + 1,), jnp.int32),
            pltpu.VMEM((GROUP, half, 2 * half), F32),
        ]

    load = jax.ShapeDtypeStruct((subs, half + rhs + 16, 2 * half), F32)
    to_sub, to_slab = pl.pallas_call(
        compose_sent,
        out_shape=(load, load),
        in_specs=[smem, smem, smem, hbm, vmem, vmem, vmem],
        out_specs=(vmem, vmem),
        scratch_shapes=scratch(2 * subs),
        name="compose_sent",
        cost_estimate=pl.CostEstimate(flops=10**9, bytes_accessed=4 * 10**6, transcendentals=0),
    )(elem_face, elem_class, partner, inv_factor, load_map, trace_map, start)

    def shifted(x, axis, up):
        last = lax.axis_size(axis) - 1
        return lax.ppermute(x, axis, [(i, i + 1) if up else (i + 1, i) for i in range(last)])

    from_slab = shifted(to_slab, "slab", False)
    from_sub = shifted(to_sub, "sub", False)

    square = jax.ShapeDtypeStruct((subs * kept, 2 * half, 2 * half), BF16)
    high, low = pl.pallas_call(
        compose_kept,
        out_shape=(square, square),
        in_specs=[smem, smem, hbm, vmem, vmem],
        out_specs=(vmem, vmem),
        scratch_shapes=scratch(subs * kept),
        name="compose_kept",
        cost_estimate=pl.CostEstimate(flops=2 * 10**9, bytes_accessed=8 * 10**6, transcendentals=0),
    )(elem_face, elem_class, inv_factor, load_map, trace_map)

    size = (ITERS + 1) * rhs
    back = jax.ShapeDtypeStruct((subs, ITERS * rhs, 2 * half), F32)
    gram, blocks, ret_sub, ret_slab = pl.pallas_call(
        krylov,
        out_shape=(
            jax.ShapeDtypeStruct((2 * rhs, 128), F32),
            jax.ShapeDtypeStruct((subs * kept, size, 2 * half), F32),
            back,
            back,
        ),
        in_specs=[smem, smem, vmem, vmem, vmem, vmem, vmem],
        out_specs=(vmem, vmem, vmem, vmem),
        scratch_shapes=[
            pltpu.VMEM((2 * subs, 2 * half, 2 * half), BF16),
            pltpu.VMEM((2 * subs, 2 * half, 2 * half), BF16),
            pltpu.VMEM((2 * subs, size, 2 * half), F32),
            pltpu.VMEM((subs * (kept + 2), rhs, 2 * half), F32),
        ],
        name="krylov",
    )(partner, partner_face, high, low, from_sub, from_slab, start)

    back_slab = shifted(ret_slab, "slab", True)
    back_sub = shifted(ret_sub, "sub", True)
    gram = summed(gram, ("sub", "slab"))

    return pl.pallas_call(
        functools.partial(finish, float(count)),
        out_shape=(
            jax.ShapeDtypeStruct(start.shape, F32),
            jax.ShapeDtypeStruct((ITERS, ITERS + 1, rhs, rhs), F32),
        ),
        in_specs=[vmem] * 5,
        out_specs=(vmem, vmem),
        scratch_shapes=[pltpu.VMEM((128, 128), F32), pltpu.VMEM((128, 128), F32)],
        name="finish",
    )(gram, blocks, back_sub, back_slab, start)


def solution(mesh):
    placed = (
        P(("slab", "sub"), None, None, None, None),
        P(("slab", "sub"), None, None, None),
        P(("slab", "sub"), None),
        P(("slab", "sub"), None),
        P(("slab", "sub"), None),
        P(("slab", "sub"), None),
        P(),
        P(),
    )
    return jax.shard_map(
        body,
        mesh=mesh,
        in_specs=placed,
        out_specs=(P(("slab", "sub"), None, None, None, None), P()),
        check_vma=False,
    )
```

time: 423 us -> 71.5 us (0.17)
  blocking collectives: 235 us -> 0 us
  matrix products: 61.2 us -> 0 us
  Pallas kernels: 0 us -> 36 us
  other arithmetic: 33.8 us -> 1.34 us
  starting transfers between devices: 43.5 us -> 14 us
  local copies, waits for them, and re-layouts: 22.5 us -> 1.42 us
  waiting for transfers between devices: 24.3 us -> 18.1 us
    psum x5 -> x0, blocking collectives: 235 us -> none  [the longest x4 193 us: body(): lax.psum((local_terms, local_inner(image_block, image_block)), ('slab', '...]
    dot_general x90 -> x0, matrix products: 60.1 us -> none  [the longest x12 12.9 us: complex_apply(): jnp.einsum(layout, matrix_real, vec_real, preferred_element_type=jnp.floa...]
    pallas_call x0 -> x4, Pallas kernels: none -> 36 us  [the longest x1 13.3 us: body(): pl.pallas_call(functools.partial(finish, float(count)), out_shape=(jax.Sh...]
    ppermute x16 -> x9, starting transfers between devices: 43.5 us -> 14 us  [the longest x4 9.7 us: shifted(): lax.ppermute(x, axis, [(i, i + 1) if up else (i + 1, i) for i in range(la...]
    another operation x30 -> x0, other arithmetic: 22 us -> none  [the longest x15 10.7 us: normalize(): low_factor = jnp.linalg.cholesky(gram_matrix)]
    gather x13 -> x0, local copies, waits for them, and re-layouts: 17.3 us -> none  [the longest x4 6.66 us: partner_traces(): picked = trace_pool[source_slot]]
    concatenate x8 -> x0, other arithmetic: 7.96 us -> none  [extended(): x = jnp.concatenate([before, x, after], axis=dim)]
    ppermute x16 -> x9, waiting for transfers between devices: 24.3 us -> 18.1 us  [the longest x5 13.2 us: summed(): received.append(lax.ppermute(x, axis, pairs))]
  transfers between devices with their start and end apart: 16 -> 9, of which waited for: 11 -> 6; matrix products, arithmetic and copies ran while one was open for 1% -> 2% of each run, Pallas kernels for 0% -> 14%
where the time goes in v1:
time: 71.5 us; the launch traced here: 71.6 us
  Pallas kernels  36 us (50%)
  waiting for transfers between devices  18.1 us (25%)
  starting transfers between devices  14 us (20%)
  local copies, waits for them, and re-layouts  1.42 us (2%)
  other arithmetic  1.34 us (2%)
  between operations  0.72 us (1%)
    pallas_call x1, Pallas kernels, body(): pl.pallas_call(functools.partial(finish, float(count)), out_shape=(jax.Sh...  13.3 us
    ppermute x5, waiting for transfers between devices, summed(): received.append(lax.ppermute(x, axis, pairs))  13.2 us
    pallas_call x1, Pallas kernels, body(): pl.pallas_call(compose_kept, out_shape=(square, square), in_specs=[smem,...  9.98 us
    ppermute x4, starting transfers between devices, shifted(): lax.ppermute(x, axis, [(i, i + 1) if up else (i + 1, i) for i in range(la...  9.7 us
    pallas_call x1, Pallas kernels, body(): pl.pallas_call(krylov, out_shape=(jax.ShapeDtypeStruct((2 * rhs, 128), F3...  6.54 us
    pallas_call x1, Pallas kernels, body(): pl.pallas_call(compose_sent, out_shape=(load, load), in_specs=[smem, smem...  6.25 us
    ppermute x4, waiting for transfers between devices, shifted(): lax.ppermute(x, axis, [(i, i + 1) if up else (i + 1, i) for i in range(la...  4.92 us
    ppermute x5, starting transfers between devices, summed(): received.append(lax.ppermute(x, axis, pairs))  4.3 us
  transfers between devices with their start and end apart: 9, of which 6 were waited for; matrix products, arithmetic and copies ran while one was open for 2% of the time, Pallas kernels for 14%

profile of v1, /device:TPU:0, one launch (start us, length us, event | category | flops | bytes accessed | tf_op | source)
XLA Modules:
  0.0 71.6 jit_solution(11451541912507849904)
XLA Ops:
  0.6 6.2 %compose_sent.1 = (f32[2,160,256]{2,1,0:T(8,128)}, f32[2,160,256]{2,1,0:T(8,128)}) custom-call(s32[2,16]{1,0:T(2,128)} %face_ref.3, s32[2,16]{1,0:T(2,128)} %class_ref.3, s32[2,6]{1,0:T(2,128)} %partner_ref.3, bf16[32,2,128,128]{3,2,1,0:T(8,128)(2,1)} %inv_ref.3, bf16[4,2,128,128]{3,2,1,0:T(8,128)(2,1)} %load_ref.3, bf16[4,2,128,128]{3,2,1,0:T(8,128)(2,1)} %trace_ref.3, ...), custom_call_target="tpu_custom_call" | custom-call | flops 1000000000 | bytes 4000000 | tf_op jit(solution)/shard_map/compose_sent/pallas_call | solution.py:346
  6.9 1.3 %collective-permute-start = (f32[2,160,256]{2,1,0:T(8,128)}, f32[2,160,256]{2,1,0:T(8,128)S(1)}, u32[]{:S(2)}, u32[]{:S(2)}) collective-permute-start(f32[2,160,256]{2,1,0:T(8,128)} %get-tuple-element.12), channel_id=1, source_target_pairs={{1,0},{2,1},{3,2},{5,4},{6,5},{7,6},{9,8},{10,9},{11,10},{13,12},{... | collective-permute-start | bytes 983048 | tf_op jit(solution)/shard_map/ppermute | solution.py:358
  8.2 1.3 %collective-permute-start.1 = (f32[2,160,256]{2,1,0:T(8,128)}, f32[2,160,256]{2,1,0:T(8,128)S(1)}, u32[]{:S(2)}, u32[]{:S(2)}) collective-permute-start(f32[2,160,256]{2,1,0:T(8,128)} %get-tuple-element.13), channel_id=1, source_target_pairs={{4,0},{8,4},{12,8},{16,12},{20,16},{24,20},{28,24},{5,1},{9,5},{13... | collective-permute-start | bytes 983048 | tf_op jit(solution)/shard_map/ppermute | solution.py:358
  9.5 10.0 %compose_kept.1 = (bf16[8,256,256]{2,1,0:T(8,128)(2,1)}, bf16[8,256,256]{2,1,0:T(8,128)(2,1)}) custom-call(s32[2,16]{1,0:T(2,128)} %face_ref.3, s32[2,16]{1,0:T(2,128)} %class_ref.3, bf16[32,2,128,128]{3,2,1,0:T(8,128)(2,1)} %inv_ref.3, bf16[4,2,128,128]{3,2,1,0:T(8,128)(2,1)} %load_ref.3, bf16[4,2,128,128]{3,2,1,0:T(8,128)(2,1)} %trace_ref.3), custom_call_target="tpu_custom_call" | custom-call | flops 2000000000 | bytes 8000000 | tf_op jit(solution)/shard_map/compose_kept/pallas_call | solution.py:364
  19.5 4.9 %collective-permute-done.1.from_slab_ref = f32[2,160,256]{2,1,0:T(8,128)S(1)} collective-permute-done((f32[2,160,256]{2,1,0:T(8,128)}, f32[2,160,256]{2,1,0:T(8,128)S(1)}, u32[]{:S(2)}, u32[]{:S(2)}) %collective-permute-start.1) | collective-permute-done | bytes 327712 | tf_op jit(solution)/shard_map/ppermute | solution.py:358
  24.4 0.7 %copy-done.1 = f32[2,160,256]{2,1,0:T(8,128)} copy-done((f32[2,160,256]{2,1,0:T(8,128)}, f32[2,160,256]{2,1,0:T(8,128)S(1)}, u32[]{:S(2)}) %copy-start.1) | copy-done | bytes 327704
  25.1 6.5 %krylov.1 = (f32[32,128]{1,0:T(8,128)}, f32[8,80,256]{2,1,0:T(8,128)}, f32[2,64,256]{2,1,0:T(8,128)}, f32[2,64,256]{2,1,0:T(8,128)}) custom-call(s32[2,6]{1,0:T(2,128)} %partner_ref.3, s32[2,6]{1,0:T(2,128)} %partner_face_ref.1, bf16[8,256,256]{2,1,0:T(8,128)(2,1)} %get-tuple-element.10.high_ref, bf16[8,256,256]{2,1,0:T(8,128)(2,1)} %get-tuple-element.11.low_ref, ...), custom_call_target="tpu_custom_call" | custom-call | tf_op jit(solution)/shard_map/krylov/pallas_call | solution.py:376
  31.7 2.2 %collective-permute-start.7 = (f32[2,64,256]{2,1,0:T(8,128)}, f32[2,64,256]{2,1,0:T(8,128)S(1)}, u32[]{:S(2)}, u32[]{:S(2)}) collective-permute-start(f32[2,64,256]{2,1,0:T(8,128)} %get-tuple-element.16), channel_id=1, source_target_pairs={{0,1},{1,2},{2,3},{4,5},{5,6},{6,7},{8,9},{9,10},{10,11},{12,13},{... | collective-permute-start | bytes 393224 | tf_op jit(solution)/shard_map/ppermute | solution.py:358
  33.8 5.0 %collective-permute-start.8 = (f32[2,64,256]{2,1,0:T(8,128)}, f32[2,64,256]{2,1,0:T(8,128)S(1)}, u32[]{:S(2)}, u32[]{:S(2)}) collective-permute-start(f32[2,64,256]{2,1,0:T(8,128)} %get-tuple-element.17), channel_id=1, source_target_pairs={{0,4},{4,8},{8,12},{12,16},{16,20},{20,24},{24,28},{1,5},{5,9},{9,... | collective-permute-start | bytes 393224 | tf_op jit(solution)/shard_map/ppermute | solution.py:358
  38.8 0.1 collective-permute-start.2
  38.9 1.4 %collective-permute-done.2 = f32[32,128]{1,0:T(8,128)S(1)} collective-permute-done((f32[32,128]{1,0:T(8,128)}, f32[32,128]{1,0:T(8,128)S(1)}, u32[]{:S(2)}, u32[]{:S(2)}) %collective-permute-start.2) | collective-permute-done | bytes 16416 | tf_op jit(solution)/shard_map/ppermute | solution.py:317
  40.3 0.7 %add.15 = f32[32,128]{1,0:T(8,128)S(1)} add(f32[32,128]{1,0:T(8,128)} %get-tuple-element.14, f32[32,128]{1,0:T(8,128)S(1)} %collective-permute-done.2) | non-fusion elementwise | flops 4096 | bytes 49152 | tf_op jit(solution)/shard_map/add | solution.py:319
  41.0 0.1 collective-permute-start.3
  41.1 3.7 %collective-permute-done.3 = f32[32,128]{1,0:T(8,128)S(1)} collective-permute-done((f32[32,128]{1,0:T(8,128)S(1)}, f32[32,128]{1,0:T(8,128)S(1)}, u32[]{:S(2)}, u32[]{:S(2)}) %collective-permute-start.3) | collective-permute-done | bytes 16416 | tf_op jit(solution)/shard_map/ppermute | solution.py:317
  44.7 2.2 %collective-permute-start.4 = (f32[32,128]{1,0:T(8,128)S(1)}, f32[32,128]{1,0:T(8,128)S(1)}, u32[]{:S(2)}, u32[]{:S(2)}) collective-permute-start(f32[32,128]{1,0:T(8,128)S(1)} %add.16), channel_id=1, source_target_pairs={{0,4},{4,0},{8,12},{12,8},{16,20},{20,16},{24,28},{28,24},{1,5},{5... | collective-permute-start | bytes 49160 | tf_op jit(solution)/shard_map/ppermute | solution.py:317
  46.9 1.7 %collective-permute-done.4 = f32[32,128]{1,0:T(8,128)S(1)} collective-permute-done((f32[32,128]{1,0:T(8,128)S(1)}, f32[32,128]{1,0:T(8,128)S(1)}, u32[]{:S(2)}, u32[]{:S(2)}) %collective-permute-start.4) | collective-permute-done | bytes 16416 | tf_op jit(solution)/shard_map/ppermute | solution.py:317
  48.7 0.7 collective-permute-start.5
  49.3 3.1 %collective-permute-done.5 = f32[32,128]{1,0:T(8,128)S(1)} collective-permute-done((f32[32,128]{1,0:T(8,128)S(1)}, f32[32,128]{1,0:T(8,128)S(1)}, u32[]{:S(2)}, u32[]{:S(2)}) %collective-permute-start.5) | collective-permute-done | bytes 16416 | tf_op jit(solution)/shard_map/ppermute | solution.py:317
  52.4 1.3 %collective-permute-start.6 = (f32[32,128]{1,0:T(8,128)S(1)}, f32[32,128]{1,0:T(8,128)S(1)}, u32[]{:S(2)}, u32[]{:S(2)}) collective-permute-start(f32[32,128]{1,0:T(8,128)S(1)} %add.18), channel_id=1, source_target_pairs={{0,16},{4,20},{8,24},{12,28},{16,0},{20,4},{24,8},{28,12},{1,17},{... | collective-permute-start | bytes 49160 | tf_op jit(solution)/shard_map/ppermute | solution.py:317
  53.7 3.3 %collective-permute-done.6 = f32[32,128]{1,0:T(8,128)S(1)} collective-permute-done((f32[32,128]{1,0:T(8,128)S(1)}, f32[32,128]{1,0:T(8,128)S(1)}, u32[]{:S(2)}, u32[]{:S(2)}) %collective-permute-start.6) | collective-permute-done | bytes 16416 | tf_op jit(solution)/shard_map/ppermute | solution.py:317
  57.0 0.6 add.19.gram_ref
  57.7 0.6 copy-done.2
  58.3 0.0 copy-done.3
  58.4 13.3 %finish.1 = (f32[2,6,2,16,128]{4,3,2,1,0:T(8,128)}, f32[4,5,16,16]{3,2,1,0:T(8,128)}) custom-call(f32[32,128]{1,0:T(8,128)} %add.19.gram_ref, f32[8,80,256]{2,1,0:T(8,128)} %get-tuple-element.15.kept_ref, f32[2,64,256]{2,1,0:T(8,128)} %copy-done.2, f32[2,64,256]{2,1,0:T(8,128)} %copy-done.3, f32[2,6,2,16,128]{4,3,2,1,0:T(8,128)} %start_ref.5), custom_call_target="tpu_custom_call" | custom-call | tf_op jit(solution)/shard_map/finish/pallas_call | solution.py:399
  (11 shorter events, 0.0 us)
Async XLA Ops:
  6.9 12.6 %collective-permute-start = (f32[2,160,256]{2,1,0:T(8,128)}, f32[2,160,256]{2,1,0:T(8,128)S(1)}, u32[]{:S(2)}, u32[]{:S(2)}) collective-permute-start(f32[2,160,256]{2,1,0:T(8,128)} %get-tuple-element.12), channel_id=1, source_target_pairs={{1,0},{2,1},{3,2},{5,4},{6,5},{7,6},{9,8},{10,9},{11,10},{13,12},{... | collective-permute-start | bytes 983048 | tf_op jit(solution)/shard_map/ppermute | solution.py:358
  8.2 16.2 %collective-permute-start.1 = (f32[2,160,256]{2,1,0:T(8,128)}, f32[2,160,256]{2,1,0:T(8,128)S(1)}, u32[]{:S(2)}, u32[]{:S(2)}) collective-permute-start(f32[2,160,256]{2,1,0:T(8,128)} %get-tuple-element.13), channel_id=1, source_target_pairs={{4,0},{8,4},{12,8},{16,12},{20,16},{24,20},{28,24},{5,1},{9,5},{13... | collective-permute-start | bytes 983048 | tf_op jit(solution)/shard_map/ppermute | solution.py:358
  19.5 4.9 %copy-start = (f32[2,160,256]{2,1,0:T(8,128)}, f32[2,160,256]{2,1,0:T(8,128)S(1)}, u32[]{:S(2)}) copy-start(f32[2,160,256]{2,1,0:T(8,128)S(1)} %collective-permute-done.from_sub_ref) | copy-start | bytes 983044
  24.4 0.7 %copy-start.1 = (f32[2,160,256]{2,1,0:T(8,128)}, f32[2,160,256]{2,1,0:T(8,128)S(1)}, u32[]{:S(2)}) copy-start(f32[2,160,256]{2,1,0:T(8,128)S(1)} %collective-permute-done.1.from_slab_ref) | copy-start | bytes 983044
  31.7 26.0 %collective-permute-start.7 = (f32[2,64,256]{2,1,0:T(8,128)}, f32[2,64,256]{2,1,0:T(8,128)S(1)}, u32[]{:S(2)}, u32[]{:S(2)}) collective-permute-start(f32[2,64,256]{2,1,0:T(8,128)} %get-tuple-element.16), channel_id=1, source_target_pairs={{0,1},{1,2},{2,3},{4,5},{5,6},{6,7},{8,9},{9,10},{10,11},{12,13},{... | collective-permute-start | bytes 393224 | tf_op jit(solution)/shard_map/ppermute | solution.py:358
  33.8 23.8 %collective-permute-start.8 = (f32[2,64,256]{2,1,0:T(8,128)}, f32[2,64,256]{2,1,0:T(8,128)S(1)}, u32[]{:S(2)}, u32[]{:S(2)}) collective-permute-start(f32[2,64,256]{2,1,0:T(8,128)} %get-tuple-element.17), channel_id=1, source_target_pairs={{0,4},{4,8},{8,12},{12,16},{16,20},{20,24},{24,28},{1,5},{5,9},{9,... | collective-permute-start | bytes 393224 | tf_op jit(solution)/shard_map/ppermute | solution.py:358
  38.8 1.5 %collective-permute-start.2 = (f32[32,128]{1,0:T(8,128)}, f32[32,128]{1,0:T(8,128)S(1)}, u32[]{:S(2)}, u32[]{:S(2)}) collective-permute-start(f32[32,128]{1,0:T(8,128)} %get-tuple-element.14), channel_id=1, source_target_pairs={{0,1},{1,0},{2,3},{3,2},{4,5},{5,4},{6,7},{7,6},{8,9},{9,8},{10,11... | collective-permute-start | bytes 49160 | tf_op jit(solution)/shard_map/ppermute | solution.py:317
  41.0 3.7 %collective-permute-start.3 = (f32[32,128]{1,0:T(8,128)S(1)}, f32[32,128]{1,0:T(8,128)S(1)}, u32[]{:S(2)}, u32[]{:S(2)}) collective-permute-start(f32[32,128]{1,0:T(8,128)S(1)} %add.15), channel_id=1, source_target_pairs={{0,2},{1,3},{2,0},{3,1},{4,6},{5,7},{6,4},{7,5},{8,10},{9,11},{10,... | collective-permute-start | bytes 49160 | tf_op jit(solution)/shard_map/ppermute | solution.py:317
  44.7 3.9 %collective-permute-start.4 = (f32[32,128]{1,0:T(8,128)S(1)}, f32[32,128]{1,0:T(8,128)S(1)}, u32[]{:S(2)}, u32[]{:S(2)}) collective-permute-start(f32[32,128]{1,0:T(8,128)S(1)} %add.16), channel_id=1, source_target_pairs={{0,4},{4,0},{8,12},{12,8},{16,20},{20,16},{24,28},{28,24},{1,5},{5... | collective-permute-start | bytes 49160 | tf_op jit(solution)/shard_map/ppermute | solution.py:317
  48.7 3.7 %collective-permute-start.5 = (f32[32,128]{1,0:T(8,128)S(1)}, f32[32,128]{1,0:T(8,128)S(1)}, u32[]{:S(2)}, u32[]{:S(2)}) collective-permute-start(f32[32,128]{1,0:T(8,128)S(1)} %add.17), channel_id=1, source_target_pairs={{0,8},{4,12},{8,0},{12,4},{16,24},{20,28},{24,16},{28,20},{1,9},{5... | collective-permute-start | bytes 49160 | tf_op jit(solution)/shard_map/ppermute | solution.py:317
  52.4 4.6 %collective-permute-start.6 = (f32[32,128]{1,0:T(8,128)S(1)}, f32[32,128]{1,0:T(8,128)S(1)}, u32[]{:S(2)}, u32[]{:S(2)}) collective-permute-start(f32[32,128]{1,0:T(8,128)S(1)} %add.18), channel_id=1, source_target_pairs={{0,16},{4,20},{8,24},{12,28},{16,0},{20,4},{24,8},{28,12},{1,17},{... | collective-permute-start | bytes 49160 | tf_op jit(solution)/shard_map/ppermute | solution.py:317
  57.6 0.7 copy-start.2
  57.7 0.7 copy-start.3

commit v2 on v1

v2 whole, which is shorter than its diff:
```python
import functools

import jax
import jax.numpy as jnp
from jax import lax
from jax.experimental import pallas as pl
from jax.experimental.pallas import tpu as pltpu
from jax.sharding import PartitionSpec as P


ITERS = 4
STEP_SCALE = 2.0**-8
INNER = (0, 1)
SHARED = (3, 5)
SENT = (2, 4)
GROUP = 4
ROWS = ((4, 1, 0), (3, 2))

F32 = jnp.float32
BF16 = jnp.bfloat16
HIGHEST = lax.Precision.HIGHEST
PARAMS = pltpu.CompilerParams(vmem_limit_bytes=24 * 2**20)


def dot(a, b, transposed=False, precision=None):
    dims = (((1,), (1 if transposed else 0,)), ((), ()))
    return lax.dot_general(a, b, dims, precision=precision, preferred_element_type=F32)


def two_parts(x):
    high = x.astype(BF16)
    return high, (x - high.astype(F32)).astype(BF16)


def doubled(x):
    return jnp.concatenate(two_parts(x), axis=0)


def embedded(real, imag):
    return jnp.concatenate(
        [jnp.concatenate([real, -imag], axis=1), jnp.concatenate([imag, real], axis=1)], axis=0
    )


def compose(faces, face_ref, class_ref, held, first_ref, last_ref, sum_ref, lists, part):
    ids, kinds, places = lists
    subs, elems = face_ref.shape
    half = held.shape[2]
    total = jnp.int32(0)
    for s in range(subs):
        for e in range(elems):
            face = face_ref[s, e]
            place = jnp.int32(s * len(faces))
            hit = face == faces[0]
            for i in range(1, len(faces)):
                hit = hit | (face == faces[i])
                place = jnp.where(face == faces[i], s * len(faces) + i, place)
            ids[total] = s * elems + e
            kinds[total] = class_ref[s, e]
            places[total] = place
            total = total + hit.astype(jnp.int32)
    sum_ref[...] = jnp.zeros_like(sum_ref)

    def group(g, carry):
        where = [jnp.minimum(g * GROUP + u, total - 1) for u in range(GROUP)]
        for u in range(GROUP):
            kind = kinds[where[u]]
            wide = embedded(held[ids[where[u]], 0], held[ids[where[u]], 1])
            out = dot(first_ref[kind], wide, True)
            out = dot(doubled(out), wide)
            out = dot(doubled(out[:half] + out[half:]), last_ref[kind], True)
            part[u] = out[:half] + out[half:]
        for u in range(GROUP):
            at = places[where[u]]
            sum_ref[at] = sum_ref[at] + jnp.where(g * GROUP + u < total, part[u], 0.0)
        return carry

    lax.fori_loop(0, (total + GROUP - 1) // GROUP, group, 0)


def pack(out_ref, sum_ref, start_of, partner_ref, face, subs):
    half = sum_ref.shape[1]
    for s in range(subs):
        real, imag = start_of(s)
        rhs = real.shape[0]
        out_ref[s, :half] = sum_ref[s]
        out_ref[s, half : half + rhs, :half] = real
        out_ref[s, half : half + rhs, half:] = imag
        partner = partner_ref[s, face]
        there = (partner >= 0).astype(F32)
        local = jnp.where(partner >= 0, partner % subs, 0).astype(F32)
        out_ref[s, half + rhs : half + rhs + 8] = jnp.full((8, 2 * half), local, F32)
        out_ref[s, half + rhs + 8 : half + rhs + 16] = jnp.full((8, 2 * half), there, F32)


def compose_slab(face_hbm, class_hbm, partner_hbm, inv_ref, load_ref, trace_ref, start_ref,
                 out_ref, held, first_ref, last_ref, sum_ref, part, ids, kinds, places,
                 load, trace, rows, face_ref, class_ref, partner_ref, sems):
    subs = face_ref.shape[0]
    half = load_ref.shape[2]
    pieces = sems.shape[0] - 6
    step = inv_ref.shape[0] // pieces
    copies = [
        pltpu.make_async_copy(load_ref, load, sems.at[0]),
        pltpu.make_async_copy(trace_ref, trace, sems.at[1]),
        pltpu.make_async_copy(start_ref.at[:, SENT[1]], rows, sems.at[2]),
    ]
    for i, (source, place) in enumerate(
        ((face_hbm, face_ref), (class_hbm, class_ref), (partner_hbm, partner_ref))
    ):
        copies.append(pltpu.make_async_copy(source, place, sems.at[3 + i]))
    for i in range(pieces):
        span = pl.ds(i * step, step)
        copies.append(pltpu.make_async_copy(inv_ref.at[span], held.at[span], sems.at[6 + i]))
    for copy in copies:
        copy.start()
    copies[0].wait()
    copies[1].wait()
    for c in range(load_ref.shape[0]):
        for x in range(2):
            first_ref[c, :, x * half : (x + 1) * half] = load[c, x].astype(F32).T.astype(BF16)
        last_ref[c] = embedded(trace[c, 0], trace[c, 1])
    for copy in copies[2:]:
        copy.wait()
    compose(SENT[1:], face_ref, class_ref, held, first_ref, last_ref, sum_ref,
            (ids, kinds, places), part)
    pack(out_ref, sum_ref, lambda s: (rows[s, 0], rows[s, 1]), partner_ref, SENT[1], subs)


def compose_sub(face_ref, class_ref, partner_ref, held, first_ref, last_ref, start_ref,
                out_ref, sum_ref, part, ids, kinds, places):
    subs = face_ref.shape[0]
    compose(SENT[:1], face_ref, class_ref, held, first_ref, last_ref, sum_ref,
            (ids, kinds, places), part)
    pack(out_ref, sum_ref, lambda s: (start_ref[s, SENT[0], 0], start_ref[s, SENT[0], 1]),
         partner_ref, SENT[0], subs)


def spread(rows):
    half = rows.shape[0]
    lower = jnp.concatenate([-rows[:, half:], rows[:, :half]], axis=1)
    return two_parts(jnp.concatenate([rows, lower], axis=0))


def leaving(high, low, x, wide_high, wide_low):
    rhs = x.shape[0]
    both = dot(jnp.concatenate([high, low], axis=0), wide_high)
    return (both[:rhs] + both[rhs:] + dot(high, wide_low) - x) * STEP_SCALE


def products(pairs):
    total = None
    for high, low in pairs:
        both = jnp.concatenate([high, low], axis=0)
        term = dot(both, both, True)
        total = term if total is None else total + term
    size = total.shape[0] // 2
    return (total[:size, :size] + total[size:, size:]) + (total[:size, size:] + total[size:, :size])


def compose_kept(face_ref, class_ref, partner_ref, partner_face_ref, held, first_ref, last_ref,
                 start_ref, wide_high, wide_low, rows_high, rows_low, gram_ref,
                 sum_ref, part, ids, kinds, places, inner_high, inner_low, now_ref, out_ref):
    subs, _, _, rhs, _ = start_ref.shape
    faces = INNER + SHARED
    inner = len(INNER)
    compose(faces, face_ref, class_ref, held, first_ref, last_ref, sum_ref,
            (ids, kinds, places), part)
    for s in range(subs):
        for i in range(len(faces)):
            high, low = spread(sum_ref[s * len(faces) + i])
            if i < inner:
                inner_high[s * inner + i] = high
                inner_low[s * inner + i] = low
            else:
                at = (i - inner) * subs + s
                wide_high[at] = high
                wide_low[at] = low
    slots = subs * inner
    for s in range(subs):
        for f in INNER:
            value = jnp.concatenate([start_ref[s, f, 0], start_ref[s, f, 1]], axis=1)
            now_ref[s * inner + f] = value
            high, low = two_parts(value)
            rows_high[s * inner + f, :rhs] = high
            rows_low[s * inner + f, :rhs] = low
    for k in range(ITERS):
        now = slice(k * rhs, (k + 1) * rhs)
        later = slice((k + 1) * rhs, (k + 2) * rhs)
        for at in range(slots):
            out_ref[at] = leaving(rows_high[at, now], rows_low[at, now], now_ref[at],
                                  inner_high[at], inner_low[at])
        for s in range(subs):
            for f in INNER:
                local = partner_ref[s, f] % subs * inner + partner_face_ref[s, f]
                value = out_ref[0]
                for p in range(1, slots):
                    value = jnp.where(local == p, out_ref[p], value)
                now_ref[s * inner + f] = value
                high, low = two_parts(value)
                rows_high[s * inner + f, later] = high
                rows_low[s * inner + f, later] = low
    size = (ITERS + 1) * rhs
    gram_ref[:, :size] = products([(rows_high[at], rows_low[at]) for at in range(slots)])


def krylov(partner_ref, wide_high, wide_low, from_sub_ref, from_slab_ref, start_ref, inner_ref,
           gram_ref, rows_high, rows_low, to_sub_ref, to_slab_ref,
           far_wide_high, far_wide_low, far_high, far_low, now_ref, out_ref):
    subs, _, _, rhs, half = start_ref.shape
    own = 2 * subs
    sources = (from_sub_ref, from_slab_ref)
    targets = (to_sub_ref, to_slab_ref)

    for d in range(2):
        for s in range(subs):
            at = d * subs + s
            face = SHARED[d]
            far_wide_high[at], far_wide_low[at] = spread(sources[d][s, :half])
            value = jnp.concatenate([start_ref[s, face, 0], start_ref[s, face, 1]], axis=1)
            now_ref[at] = value
            rows_high[at, :rhs], rows_low[at, :rhs] = two_parts(value)
            value = sources[d][s, half : half + rhs]
            now_ref[own + at] = value
            far_high[at, :rhs], far_low[at, :rhs] = two_parts(value)

    for k in range(ITERS):
        now = slice(k * rhs, (k + 1) * rhs)
        later = slice((k + 1) * rhs, (k + 2) * rhs)
        for at in range(own):
            out_ref[at] = leaving(rows_high[at, now], rows_low[at, now], now_ref[at],
                                  wide_high[at], wide_low[at])
            out_ref[own + at] = leaving(far_high[at, now], far_low[at, now], now_ref[own + at],
                                        far_wide_high[at], far_wide_low[at])
        for d in range(2):
            for s in range(subs):
                at = d * subs + s
                partner = partner_ref[s, SHARED[d]]
                local = partner % subs
                value = out_ref[own + d * subs]
                for p in range(1, subs):
                    value = jnp.where(local == p, out_ref[own + d * subs + p], value)
                value = jnp.where(partner >= 0, value, 0.0)
                now_ref[at] = value
                rows_high[at, later], rows_low[at, later] = two_parts(value)
                local = sources[d][s, half + rhs : half + rhs + 1]
                there = sources[d][s, half + rhs + 8 : half + rhs + 9]
                value = out_ref[d * subs]
                for p in range(1, subs):
                    value = jnp.where(local > p - 0.5, out_ref[d * subs + p], value)
                value = jnp.where(there > 0.5, value, 0.0)
                now_ref[own + at] = value
                far_high[at, later], far_low[at, later] = two_parts(value)
                targets[d][s, now] = value

    size = (ITERS + 1) * rhs
    total = inner_ref[:, :size] + products(
        [(rows_high[at], rows_low[at]) for at in range(own)]
        + [(far_high[at], far_low[at]) for at in range(own)]
    )
    alone = []
    for face in SENT:
        for s in range(subs):
            share = jnp.where(partner_ref[s, face] < 0, 1.0, 0.0)
            rows = jnp.concatenate([start_ref[s, face, 0], start_ref[s, face, 1]], axis=1)
            alone.append(two_parts(rows * share))
    first = total[:rhs, :rhs] + products(alone)

    gram_ref[...] = jnp.zeros_like(gram_ref)
    for row, blocks in enumerate(ROWS):
        lane = 0
        for i in blocks:
            width = (i + 1) * rhs
            piece = first if i == 0 else total[i * rhs : (i + 1) * rhs, :width]
            gram_ref[row * rhs : (row + 1) * rhs, lane : lane + width] = piece
            lane += width


def finish(count, gram_ref, inner_high, inner_low, rows_high, rows_low, back_sub_ref,
           back_slab_ref, start_ref, last_ref, hess_ref, upper_ref, inverse_ref, back_high, back_low):
    subs, _, _, rhs, half = start_ref.shape
    size = (ITERS + 1) * rhs
    lanes = 128
    for d, back_ref in enumerate((back_sub_ref, back_slab_ref)):
        for s in range(subs):
            at = d * subs + s
            first = jnp.concatenate([start_ref[s, SENT[d], 0], start_ref[s, SENT[d], 1]], axis=1)
            back_high[at, :rhs], back_low[at, :rhs] = two_parts(first)
            back_high[at, rhs:], back_low[at, rhs:] = two_parts(back_ref[s])

    upper_ref[...] = jnp.zeros_like(upper_ref)
    for row, blocks in enumerate(ROWS):
        lane = 0
        for i in blocks:
            width = (i + 1) * rhs
            upper_ref[i * rhs : (i + 1) * rhs, :width] = (
                gram_ref[row * rhs : (row + 1) * rhs, lane : lane + width] / count
            )
            lane += width
    lower = upper_ref[...]
    down = lax.broadcasted_iota(jnp.int32, (lanes, lanes), 0)
    across = lax.broadcasted_iota(jnp.int32, (lanes, lanes), 1)
    full = jnp.where(down >= across, lower, lower.T)

    blocks = size // 8
    work = [full[8 * i : 8 * i + 8] for i in range(blocks)]
    side = [
        (down[8 * i : 8 * i + 8] == across[8 * i : 8 * i + 8]).astype(F32) for i in range(blocks)
    ]
    sub_row = lax.broadcasted_iota(jnp.int32, (8, lanes), 0)

    def spread_row(x, r):
        return jnp.broadcast_to(x[r : r + 1], (8, lanes))

    for i in range(blocks):
        columns = {
            m: [jnp.broadcast_to(work[m][:, 8 * i + q : 8 * i + q + 1], (8, lanes)) for q in range(8)]
            for m in range(i, blocks)
        }
        own = list(columns[i])
        row, other = work[i], side[i]
        for r in range(8):
            pivot = spread_row(own[r], r)
            root = lax.rsqrt(pivot)
            scale = 1.0 / pivot
            chosen = sub_row == r
            factor = own[r]
            top, rest = spread_row(row, r), spread_row(other, r)
            j = 8 * i + r
            upper_ref[j : j + 1, :] = (top * root)[:1]
            inverse_ref[j : j + 1, :] = (rest * root)[:1]

            def cleared(x, x_row):
                x_row = x_row * scale
                return jnp.where(chosen, x_row, x - factor * x_row)

            row, other = cleared(row, top), cleared(other, rest)
            for q in range(r + 1, 8):
                own[q] = cleared(own[q], spread_row(own[q], r))
        tops = [spread_row(row, q) for q in range(8)]
        rests = [spread_row(other, q) for q in range(8)]
        for m in range(i + 1, blocks):
            terms = [columns[m][q] * tops[q] for q in range(8)]
            while len(terms) > 1:
                terms = [terms[q] + terms[q + 1] for q in range(0, len(terms), 2)]
            work[m] = work[m] - terms[0]
            terms = [columns[m][q] * rests[q] for q in range(8)]
            while len(terms) > 1:
                terms = [terms[q] + terms[q + 1] for q in range(0, len(terms), 2)]
            side[m] = side[m] - terms[0]
    upper_ref[size:, :] = jnp.zeros((lanes - size, lanes), F32)
    inverse_ref[size:, :] = jnp.zeros((lanes - size, lanes), F32)

    upper = jnp.where(down <= across, upper_ref[...], 0.0)
    inverse = jnp.where(down >= across, inverse_ref[...], 0.0)
    mix = inverse[ITERS * rhs : size, :size]
    mix_high, mix_low = two_parts(mix)
    mix_both = jnp.concatenate([mix_high, mix_low], axis=0)

    def put(s, face, high, low):
        value = dot(mix_both, high)
        value = value[:rhs] + value[rhs:] + dot(mix_high, low)
        last_ref[s, face, 0] = value[:, :half]
        last_ref[s, face, 1] = value[:, half:]

    for s in range(subs):
        for f in INNER:
            at = s * len(INNER) + f
            put(s, f, inner_high[at], inner_low[at])
        for d in range(2):
            at = d * subs + s
            put(s, SHARED[d], rows_high[at], rows_low[at])
            put(s, SENT[d], back_high[at], back_low[at])

    shifted = jnp.concatenate([upper[:, rhs:], jnp.zeros((lanes, rhs), F32)], axis=1)
    moved = dot(shifted, inverse, True, HIGHEST) * (1.0 / STEP_SCALE)
    unit = (down[:rhs, :rhs] == across[:rhs, :rhs]).astype(F32)
    for k in range(ITERS):
        for j in range(ITERS + 1):
            if j > k + 1:
                hess_ref[k, j] = jnp.zeros((rhs, rhs), F32)
                continue
            block = moved[j * rhs : (j + 1) * rhs, k * rhs : (k + 1) * rhs]
            block = block if (j + k) % 2 else -block
            hess_ref[k, j] = block + unit if j == k else block


def summed(x, axes):
    for axis in axes:
        count, stride = lax.axis_size(axis), 1
        while stride < count:
            rest = count // stride
            ways = next(p for p in range(2, rest + 1) if rest % p == 0)
            received = []
            for d in range(1, ways):
                pairs = []
                for i in range(count):
                    digit = (i // stride) % ways
                    pairs.append((i, i + ((digit + d) % ways - digit) * stride))
                received.append(lax.ppermute(x, axis, pairs))
            for y in received:
                x = x + y
            stride *= ways
    return x


def body(start, inv_factor, partner, partner_face, elem_class, elem_face, load_map, trace_map):
    subs, _, _, rhs, half = start.shape
    elems = elem_class.shape[1]
    classes = load_map.shape[0]
    count = start.size // rhs * lax.axis_size("slab") * lax.axis_size("sub")
    size = (ITERS + 1) * rhs
    full = 2 * half
    smem = pl.BlockSpec(memory_space=pltpu.SMEM)
    vmem = pl.BlockSpec(memory_space=pltpu.VMEM)
    hbm = pl.BlockSpec(memory_space=pltpu.HBM)

    def shape(*dims, dtype=F32):
        return jax.ShapeDtypeStruct(dims, dtype)

    def scratch(sums):
        return [
            pltpu.VMEM((sums, half, full), F32),
            pltpu.VMEM((GROUP, half, full), F32),
            pltpu.SMEM((subs * elems + 1,), jnp.int32),
            pltpu.SMEM((subs * elems + 1,), jnp.int32),
            pltpu.SMEM((subs * elems + 1,), jnp.int32),
        ]

    def call(kernel, out_shape, in_specs, scratch_shapes):
        return pl.pallas_call(
            kernel,
            out_shape=out_shape,
            in_specs=in_specs,
            out_specs=(vmem,) * len(out_shape),
            scratch_shapes=scratch_shapes,
            compiler_params=PARAMS,
            cost_estimate=pl.CostEstimate(
                flops=2 * 10**9, bytes_accessed=4 * 10**6, transcendentals=0
            ),
        )

    def shifted(x, axis, up):
        last = lax.axis_size(axis) - 1
        return lax.ppermute(x, axis, [(i, i + 1) if up else (i + 1, i) for i in range(last)])

    load = shape(subs, half + rhs + 16, full)
    far = [
        pltpu.with_memory_space_constraint(x, pltpu.HBM)
        for x in (elem_face, elem_class, partner, inv_factor, load_map, trace_map, start)
    ]
    to_slab, held, first, last = call(
        compose_slab,
        (load, shape(*inv_factor.shape, dtype=BF16), shape(classes, half, full, dtype=BF16),
         shape(classes, full, full, dtype=BF16)),
        [hbm] * 7,
        scratch(subs) + [
            pltpu.VMEM(load_map.shape, BF16),
            pltpu.VMEM(trace_map.shape, BF16),
            pltpu.VMEM((subs, 2, rhs, half), F32),
            pltpu.SMEM(elem_face.shape, jnp.int32),
            pltpu.SMEM(elem_class.shape, jnp.int32),
            pltpu.SMEM(partner.shape, jnp.int32),
            pltpu.SemaphoreType.DMA((6 + 4,)),
        ],
    )(*far)
    from_slab = shifted(to_slab, "slab", False)

    (to_sub,) = call(
        compose_sub, (load,), [smem, smem, smem] + [vmem] * 4, scratch(subs)
    )(elem_face, elem_class, partner, held, first, last, start)
    from_sub = shifted(to_sub, "sub", False)

    slots = 2 * subs
    square = shape(slots, full, full, dtype=BF16)
    rows = shape(slots, size, full, dtype=BF16)
    wide_high, wide_low, inner_high, inner_low, inner_gram = call(
        compose_kept,
        (square, square, rows, rows, shape(size, 128)),
        [smem, smem, smem, smem] + [vmem] * 4,
        scratch(2 * slots) + [
            pltpu.VMEM((slots, full, full), BF16),
            pltpu.VMEM((slots, full, full), BF16),
            pltpu.VMEM((slots, rhs, full), F32),
            pltpu.VMEM((slots, rhs, full), F32),
        ],
    )(elem_face, elem_class, partner, partner_face, held, first, last, start)

    back = shape(subs, ITERS * rhs, full)
    gram, rows_high, rows_low, ret_sub, ret_slab = call(
        krylov,
        (shape(2 * rhs, 128), rows, rows, back, back),
        [smem] + [vmem] * 6,
        [
            pltpu.VMEM((slots, full, full), BF16),
            pltpu.VMEM((slots, full, full), BF16),
            pltpu.VMEM((slots, size, full), BF16),
            pltpu.VMEM((slots, size, full), BF16),
            pltpu.VMEM((2 * slots, rhs, full), F32),
            pltpu.VMEM((2 * slots, rhs, full), F32),
        ],
    )(partner, wide_high, wide_low, from_sub, from_slab, start, inner_gram)

    back_slab = shifted(ret_slab, "slab", True)
    back_sub = shifted(ret_sub, "sub", True)
    gram = summed(gram, ("sub", "slab"))

    return call(
        functools.partial(finish, float(count)),
        (shape(*start.shape), shape(ITERS, ITERS + 1, rhs, rhs)),
        [vmem] * 8,
        [
            pltpu.VMEM((128, 128), F32),
            pltpu.VMEM((128, 128), F32),
            pltpu.VMEM((slots, size, full), BF16),
            pltpu.VMEM((slots, size, full), BF16),
        ],
    )(gram, inner_high, inner_low, rows_high, rows_low, back_sub, back_slab, start)


def solution(mesh):
    placed = (
        P(("slab", "sub"), None, None, None, None),
        P(("slab", "sub"), None, None, None),
        P(("slab", "sub"), None),
        P(("slab", "sub"), None),
        P(("slab", "sub"), None),
        P(("slab", "sub"), None),
        P(),
        P(),
    )

    return jax.shard_map(
        body,
        mesh=mesh,
        in_specs=placed,
        out_specs=(P(("slab", "sub"), None, None, None, None), P()),
        check_vma=False,
    )
```

time: 71.5 us -> 53.5 us (0.75)
  Pallas kernels: 36 us -> 20.5 us
  waiting for transfers between devices: 18.1 us -> 15.2 us
  starting transfers between devices: 14 us -> 16.7 us
  local copies, waits for them, and re-layouts: 1.42 us -> 0.02 us
  other arithmetic: 1.34 us -> 0.02 us
    pallas_call x4 -> x5, Pallas kernels: 36 us -> 20.5 us  [the longest x1 6.36 us: body(): call(compose_kept, (square, square, rows, rows, shape(size, 128)), [smem,...]
    ppermute x5, starting transfers between devices: 4.3 us -> 8.79 us  [summed(): received.append(lax.ppermute(x, axis, pairs))]
    ppermute x5, waiting for transfers between devices: 13.2 us -> 10.6 us  [summed(): received.append(lax.ppermute(x, axis, pairs))]
    ppermute x4, starting transfers between devices: 9.7 us -> 7.9 us  [shifted(): lax.ppermute(x, axis, [(i, i + 1) if up else (i + 1, i) for i in range(la...]
    unnamed x8 -> x10, local copies, waits for them, and re-layouts: 1.42 us -> 0.02 us
    add x5, other arithmetic: 1.34 us -> 0.02 us  [summed(): x = x + y]
  transfers between devices with their start and end apart: 9 -> 9, of which waited for: 6 -> 6; matrix products, arithmetic and copies ran while one was open for 2% -> 0% of each run, Pallas kernels for 14% -> 12%
where the time goes in v2:
time: 53.5 us; the launch traced here: 53.3 us
  Pallas kernels  20.5 us (38%)
  starting transfers between devices  16.7 us (31%)
  waiting for transfers between devices  15.2 us (28%)
  between operations  0.79 us (1%)
    ppermute x5, waiting for transfers between devices, summed(): received.append(lax.ppermute(x, axis, pairs))  10.6 us
    ppermute x5, starting transfers between devices, summed(): received.append(lax.ppermute(x, axis, pairs))  8.79 us
    ppermute x4, starting transfers between devices, shifted(): lax.ppermute(x, axis, [(i, i + 1) if up else (i + 1, i) for i in range(la...  7.9 us
    pallas_call x1, Pallas kernels, body(): call(compose_kept, (square, square, rows, rows, shape(size, 128)), [smem,...  6.36 us
    pallas_call x1, Pallas kernels, body(): call(compose_slab, (load, shape(*inv_factor.shape, dtype=BF16), shape(cla...  4.99 us
    ppermute x4, waiting for transfers between devices, shifted(): lax.ppermute(x, axis, [(i, i + 1) if up else (i + 1, i) for i in range(la...  4.64 us
    pallas_call x1, Pallas kernels, body(): call(functools.partial(finish, float(count)), (shape(*start.shape), shape...  3.99 us
    pallas_call x1, Pallas kernels, body(): call(compose_sub, (load,), [smem, smem, smem] + [vmem] * 4, scratch(subs))  2.71 us
  transfers between devices with their start and end apart: 9, of which 6 were waited for; matrix products, arithmetic and copies ran while one was open for 0% of the time, Pallas kernels for 12%

profile of v2, /device:TPU:0, one launch (start us, length us, event | category | flops | bytes accessed | tf_op | source)
XLA Modules:
  0.0 53.3 jit_solution(16515358847485974132)
XLA Ops:
  0.7 5.0 %shard_map.95 = (f32[2,160,256]{2,1,0:T(8,128)S(1)}, bf16[32,2,128,128]{3,2,1,0:T(8,128)(2,1)S(1)}, bf16[4,128,256]{2,1,0:T(8,128)(2,1)S(1)}, bf16[4,256,256]{2,1,0:T(8,128)(2,1)S(1)}) custom-call(s32[2,16]{1,0:T(2,128)} %face_ref.3, s32[2,16]{1,0:T(2,128)} %class_ref.3, s32[2,6]{1,0:T(2,128)} %partner_ref.5, bf16[32,2,128,128]{3,2,1,0:T(8,128)(2,1)} %inv_ref.1, ...), custom_call_target="tpu_custom_call" | custom-call | flops 2000000000 | bytes 4000000 | tf_op jit(solution)/shard_map/pallas_call | solution.py:452
  5.7 0.0 copy-start.3
  5.7 2.7 %shard_map.97 = f32[2,160,256]{2,1,0:T(8,128)S(1)} custom-call(s32[2,16]{1,0:T(2,128)S(1)} %copy-done.1, s32[2,16]{1,0:T(2,128)S(1)} %copy-done.2, s32[2,6]{1,0:T(2,128)S(1)} %copy-done.4, bf16[32,2,128,128]{3,2,1,0:T(8,128)(2,1)S(1)} %get-tuple-element.16.held, bf16[4,128,256]{2,1,0:T(8,128)(2,1)S(1)} %get-tuple-element.17.first_ref, ...), custom_call_target="tpu_custom_call" | custom-call | flops 2000000000 | bytes 4000000 | tf_op jit(solution)/shard_map/pallas_call | solution.py:469
  8.4 1.3 %collective-permute-start = (f32[2,160,256]{2,1,0:T(8,128)S(1)}, f32[2,160,256]{2,1,0:T(8,128)S(1)}, u32[]{:S(2)}, u32[]{:S(2)}) collective-permute-start(f32[2,160,256]{2,1,0:T(8,128)S(1)} %shard_map.97), channel_id=1, source_target_pairs={{1,0},{2,1},{3,2},{5,4},{6,5},{7,6},{9,8},{10,9},{11,10},{13,12},{... | collective-permute-start | bytes 983048 | tf_op jit(solution)/shard_map/ppermute | solution.py:445
  9.7 1.3 %collective-permute-start.1 = (f32[2,160,256]{2,1,0:T(8,128)S(1)}, f32[2,160,256]{2,1,0:T(8,128)S(1)}, u32[]{:S(2)}, u32[]{:S(2)}) collective-permute-start(f32[2,160,256]{2,1,0:T(8,128)S(1)} %get-tuple-element.21), channel_id=1, source_target_pairs={{4,0},{8,4},{12,8},{16,12},{20,16},{24,20},{28,24},{5,1},{9,5},{13... | collective-permute-start | bytes 983048 | tf_op jit(solution)/shard_map/ppermute | solution.py:445
  11.1 6.4 %shard_map.96 = (bf16[4,256,256]{2,1,0:T(8,128)(2,1)S(1)}, bf16[4,256,256]{2,1,0:T(8,128)(2,1)S(1)}, bf16[4,80,256]{2,1,0:T(8,128)(2,1)S(1)}, bf16[4,80,256]{2,1,0:T(8,128)(2,1)S(1)}, f32[80,128]{1,0:T(8,128)S(1)}) custom-call(s32[2,16]{1,0:T(2,128)S(1)} %copy-done.1, s32[2,16]{1,0:T(2,128)S(1)} %copy-done.2, s32[2,6]{1,0:T(2,128)S(1)} %copy-done.4, ...), custom_call_target="tpu_custom_call" | custom-call | flops 2000000000 | bytes 4000000 | tf_op jit(solution)/shard_map/pallas_call | solution.py:477
  17.4 0.0 collective-permute-done.from_sub_ref
  17.4 4.6 %collective-permute-done.1.from_slab_ref = f32[2,160,256]{2,1,0:T(8,128)S(1)} collective-permute-done((f32[2,160,256]{2,1,0:T(8,128)S(1)}, f32[2,160,256]{2,1,0:T(8,128)S(1)}, u32[]{:S(2)}, u32[]{:S(2)}) %collective-permute-start.1) | collective-permute-done | bytes 327712 | tf_op jit(solution)/shard_map/ppermute | solution.py:445
  22.1 2.5 %shard_map.98 = (f32[32,128]{1,0:T(8,128)S(1)}, bf16[4,80,256]{2,1,0:T(8,128)(2,1)S(1)}, bf16[4,80,256]{2,1,0:T(8,128)(2,1)S(1)}, f32[2,64,256]{2,1,0:T(8,128)S(1)}, f32[2,64,256]{2,1,0:T(8,128)S(1)}) custom-call(s32[2,6]{1,0:T(2,128)S(1)} %copy-done.4, bf16[4,256,256]{2,1,0:T(8,128)(2,1)S(1)} %get-tuple-element.19.wide_high, ...), custom_call_target="tpu_custom_call" | custom-call | flops 2000000000 | bytes 4000000 | tf_op jit(solution)/shard_map/pallas_call | solution.py:490
  24.5 2.0 %collective-permute-start.7 = (f32[2,64,256]{2,1,0:T(8,128)S(1)}, f32[2,64,256]{2,1,0:T(8,128)S(1)}, u32[]{:S(2)}, u32[]{:S(2)}) collective-permute-start(f32[2,64,256]{2,1,0:T(8,128)S(1)} %get-tuple-element.28), channel_id=1, source_target_pairs={{0,1},{1,2},{2,3},{4,5},{5,6},{6,7},{8,9},{9,10},{10,11},{12,13},{... | collective-permute-start | bytes 393224 | tf_op jit(solution)/shard_map/ppermute | solution.py:445
  26.6 3.3 %collective-permute-start.8 = (f32[2,64,256]{2,1,0:T(8,128)S(1)}, f32[2,64,256]{2,1,0:T(8,128)S(1)}, u32[]{:S(2)}, u32[]{:S(2)}) collective-permute-start(f32[2,64,256]{2,1,0:T(8,128)S(1)} %get-tuple-element.29), channel_id=1, source_target_pairs={{0,4},{4,8},{8,12},{12,16},{16,20},{20,24},{24,28},{1,5},{5,9},{9,... | collective-permute-start | bytes 393224 | tf_op jit(solution)/shard_map/ppermute | solution.py:445
  29.9 2.0 %collective-permute-start.2 = (f32[32,128]{1,0:T(8,128)S(1)}, f32[32,128]{1,0:T(8,128)S(1)}, u32[]{:S(2)}, u32[]{:S(2)}) collective-permute-start(f32[32,128]{1,0:T(8,128)S(1)} %get-tuple-element.23), channel_id=1, source_target_pairs={{0,1},{1,0},{2,3},{3,2},{4,5},{5,4},{6,7},{7,6},{8,9},{9,8},{10,11... | collective-permute-start | bytes 49160 | tf_op jit(solution)/shard_map/ppermute | solution.py:400
  31.9 0.8 %collective-permute-done.2 = f32[32,128]{1,0:T(8,128)S(1)} collective-permute-done((f32[32,128]{1,0:T(8,128)S(1)}, f32[32,128]{1,0:T(8,128)S(1)}, u32[]{:S(2)}, u32[]{:S(2)}) %collective-permute-start.2) | collective-permute-done | bytes 16416 | tf_op jit(solution)/shard_map/ppermute | solution.py:400
  32.7 0.5 collective-permute-start.3
  33.2 3.2 %collective-permute-done.3 = f32[32,128]{1,0:T(8,128)S(1)} collective-permute-done((f32[32,128]{1,0:T(8,128)S(1)}, f32[32,128]{1,0:T(8,128)S(1)}, u32[]{:S(2)}, u32[]{:S(2)}) %collective-permute-start.3) | collective-permute-done | bytes 16416 | tf_op jit(solution)/shard_map/ppermute | solution.py:400
  36.5 1.5 %collective-permute-start.4 = (f32[32,128]{1,0:T(8,128)S(1)}, f32[32,128]{1,0:T(8,128)S(1)}, u32[]{:S(2)}, u32[]{:S(2)}) collective-permute-start(f32[32,128]{1,0:T(8,128)S(1)} %add.16), channel_id=1, source_target_pairs={{0,4},{4,0},{8,12},{12,8},{16,20},{20,16},{24,28},{28,24},{1,5},{5... | collective-permute-start | bytes 49160 | tf_op jit(solution)/shard_map/ppermute | solution.py:400
  38.0 2.2 %collective-permute-done.4 = f32[32,128]{1,0:T(8,128)S(1)} collective-permute-done((f32[32,128]{1,0:T(8,128)S(1)}, f32[32,128]{1,0:T(8,128)S(1)}, u32[]{:S(2)}, u32[]{:S(2)}) %collective-permute-start.4) | collective-permute-done | bytes 16416 | tf_op jit(solution)/shard_map/ppermute | solution.py:400
  40.2 2.7 %collective-permute-start.5 = (f32[32,128]{1,0:T(8,128)S(1)}, f32[32,128]{1,0:T(8,128)S(1)}, u32[]{:S(2)}, u32[]{:S(2)}) collective-permute-start(f32[32,128]{1,0:T(8,128)S(1)} %add.17), channel_id=1, source_target_pairs={{0,8},{4,12},{8,0},{12,4},{16,24},{20,28},{24,16},{28,20},{1,9},{5... | collective-permute-start | bytes 49160 | tf_op jit(solution)/shard_map/ppermute | solution.py:400
  42.9 1.7 %collective-permute-done.5 = f32[32,128]{1,0:T(8,128)S(1)} collective-permute-done((f32[32,128]{1,0:T(8,128)S(1)}, f32[32,128]{1,0:T(8,128)S(1)}, u32[]{:S(2)}, u32[]{:S(2)}) %collective-permute-start.5) | collective-permute-done | bytes 16416 | tf_op jit(solution)/shard_map/ppermute | solution.py:400
  44.6 2.0 %collective-permute-start.6 = (f32[32,128]{1,0:T(8,128)S(1)}, f32[32,128]{1,0:T(8,128)S(1)}, u32[]{:S(2)}, u32[]{:S(2)}) collective-permute-start(f32[32,128]{1,0:T(8,128)S(1)} %add.18), channel_id=1, source_target_pairs={{0,16},{4,20},{8,24},{12,28},{16,0},{20,4},{24,8},{28,12},{1,17},{... | collective-permute-start | bytes 49160 | tf_op jit(solution)/shard_map/ppermute | solution.py:400
  46.7 2.6 %collective-permute-done.6 = f32[32,128]{1,0:T(8,128)S(1)} collective-permute-done((f32[32,128]{1,0:T(8,128)S(1)}, f32[32,128]{1,0:T(8,128)S(1)}, u32[]{:S(2)}, u32[]{:S(2)}) %collective-permute-start.6) | collective-permute-done | bytes 16416 | tf_op jit(solution)/shard_map/ppermute | solution.py:400
  49.3 0.0 collective-permute-done.7.back_sub_ref
  49.3 0.0 collective-permute-done.8.back_slab_ref
  49.3 4.0 %shard_map.99 = (f32[2,6,2,16,128]{4,3,2,1,0:T(8,128)}, f32[4,5,16,16]{3,2,1,0:T(8,128)}) custom-call(f32[32,128]{1,0:T(8,128)S(1)} %add.19.gram_ref, bf16[4,80,256]{2,1,0:T(8,128)(2,1)S(1)} %get-tuple-element.24.inner_high, bf16[4,80,256]{2,1,0:T(8,128)(2,1)S(1)} %get-tuple-element.25.inner_low, bf16[4,80,256]{2,1,0:T(8,128)(2,1)S(1)} %get-tuple-element.26.rows_high, ...), custom_call_target="tpu_custom_call" | custom-call | flops 2000000000 | bytes 4000000 | tf_op jit(solution)/shard_map/pallas_call | solution.py:508
  (14 shorter events, 0.0 us)
Async XLA Ops:
  0.6 5.0 %copy-start = (f32[2,6,2,16,128]{4,3,2,1,0:T(8,128)S(1)}, f32[2,6,2,16,128]{4,3,2,1,0:T(8,128)}, u32[]{:S(2)}) copy-start(f32[2,6,2,16,128]{4,3,2,1,0:T(8,128)} %start_ref.9) | copy-start | bytes 589828
  0.6 5.0 %copy-start.4 = (s32[2,6]{1,0:T(2,128)S(1)}, s32[2,6]{1,0:T(2,128)}, u32[]{:S(2)}) copy-start(s32[2,6]{1,0:T(2,128)} %partner_ref.5) | copy-start | bytes 148
  0.7 5.0 %copy-start.1 = (s32[2,16]{1,0:T(2,128)S(1)}, s32[2,16]{1,0:T(2,128)}, u32[]{:S(2)}) copy-start(s32[2,16]{1,0:T(2,128)} %face_ref.3) | copy-start | bytes 388
  0.7 5.0 %copy-start.2 = (s32[2,16]{1,0:T(2,128)S(1)}, s32[2,16]{1,0:T(2,128)}, u32[]{:S(2)}) copy-start(s32[2,16]{1,0:T(2,128)} %class_ref.3) | copy-start | bytes 388
  5.7 5.3 %copy-start.3 = (s32[2,6]{1,0:T(2,128)S(1)}, s32[2,6]{1,0:T(2,128)}, u32[]{:S(2)}) copy-start(s32[2,6]{1,0:T(2,128)} %partner_face_ref.1) | copy-start | bytes 148
  8.4 9.0 %collective-permute-start = (f32[2,160,256]{2,1,0:T(8,128)S(1)}, f32[2,160,256]{2,1,0:T(8,128)S(1)}, u32[]{:S(2)}, u32[]{:S(2)}) collective-permute-start(f32[2,160,256]{2,1,0:T(8,128)S(1)} %shard_map.97), channel_id=1, source_target_pairs={{1,0},{2,1},{3,2},{5,4},{6,5},{7,6},{9,8},{10,9},{11,10},{13,12},{... | collective-permute-start | bytes 983048 | tf_op jit(solution)/shard_map/ppermute | solution.py:445
  9.7 12.3 %collective-permute-start.1 = (f32[2,160,256]{2,1,0:T(8,128)S(1)}, f32[2,160,256]{2,1,0:T(8,128)S(1)}, u32[]{:S(2)}, u32[]{:S(2)}) collective-permute-start(f32[2,160,256]{2,1,0:T(8,128)S(1)} %get-tuple-element.21), channel_id=1, source_target_pairs={{4,0},{8,4},{12,8},{16,12},{20,16},{24,20},{28,24},{5,1},{9,5},{13... | collective-permute-start | bytes 983048 | tf_op jit(solution)/shard_map/ppermute | solution.py:445
  24.5 24.7 %collective-permute-start.7 = (f32[2,64,256]{2,1,0:T(8,128)S(1)}, f32[2,64,256]{2,1,0:T(8,128)S(1)}, u32[]{:S(2)}, u32[]{:S(2)}) collective-permute-start(f32[2,64,256]{2,1,0:T(8,128)S(1)} %get-tuple-element.28), channel_id=1, source_target_pairs={{0,1},{1,2},{2,3},{4,5},{5,6},{6,7},{8,9},{9,10},{10,11},{12,13},{... | collective-permute-start | bytes 393224 | tf_op jit(solution)/shard_map/ppermute | solution.py:445
  26.6 22.7 %collective-permute-start.8 = (f32[2,64,256]{2,1,0:T(8,128)S(1)}, f32[2,64,256]{2,1,0:T(8,128)S(1)}, u32[]{:S(2)}, u32[]{:S(2)}) collective-permute-start(f32[2,64,256]{2,1,0:T(8,128)S(1)} %get-tuple-element.29), channel_id=1, source_target_pairs={{0,4},{4,8},{8,12},{12,16},{16,20},{20,24},{24,28},{1,5},{5,9},{9,... | collective-permute-start | bytes 393224 | tf_op jit(solution)/shard_map/ppermute | solution.py:445
  29.9 2.9 %collective-permute-start.2 = (f32[32,128]{1,0:T(8,128)S(1)}, f32[32,128]{1,0:T(8,128)S(1)}, u32[]{:S(2)}, u32[]{:S(2)}) collective-permute-start(f32[32,128]{1,0:T(8,128)S(1)} %get-tuple-element.23), channel_id=1, source_target_pairs={{0,1},{1,0},{2,3},{3,2},{4,5},{5,4},{6,7},{7,6},{8,9},{9,8},{10,11... | collective-permute-start | bytes 49160 | tf_op jit(solution)/shard_map/ppermute | solution.py:400
  32.7 3.7 %collective-permute-start.3 = (f32[32,128]{1,0:T(8,128)S(1)}, f32[32,128]{1,0:T(8,128)S(1)}, u32[]{:S(2)}, u32[]{:S(2)}) collective-permute-start(f32[32,128]{1,0:T(8,128)S(1)} %add.15), channel_id=1, source_target_pairs={{0,2},{1,3},{2,0},{3,1},{4,6},{5,7},{6,4},{7,5},{8,10},{9,11},{10,... | collective-permute-start | bytes 49160 | tf_op jit(solution)/shard_map/ppermute | solution.py:400
  36.5 3.7 %collective-permute-start.4 = (f32[32,128]{1,0:T(8,128)S(1)}, f32[32,128]{1,0:T(8,128)S(1)}, u32[]{:S(2)}, u32[]{:S(2)}) collective-permute-start(f32[32,128]{1,0:T(8,128)S(1)} %add.16), channel_id=1, source_target_pairs={{0,4},{4,0},{8,12},{12,8},{16,20},{20,16},{24,28},{28,24},{1,5},{5... | collective-permute-start | bytes 49160 | tf_op jit(solution)/shard_map/ppermute | solution.py:400
  40.2 4.4 %collective-permute-start.5 = (f32[32,128]{1,0:T(8,128)S(1)}, f32[32,128]{1,0:T(8,128)S(1)}, u32[]{:S(2)}, u32[]{:S(2)}) collective-permute-start(f32[32,128]{1,0:T(8,128)S(1)} %add.17), channel_id=1, source_target_pairs={{0,8},{4,12},{8,0},{12,4},{16,24},{20,28},{24,16},{28,20},{1,9},{5... | collective-permute-start | bytes 49160 | tf_op jit(solution)/shard_map/ppermute | solution.py:400
  44.6 4.6 %collective-permute-start.6 = (f32[32,128]{1,0:T(8,128)S(1)}, f32[32,128]{1,0:T(8,128)S(1)}, u32[]{:S(2)}, u32[]{:S(2)}) collective-permute-start(f32[32,128]{1,0:T(8,128)S(1)} %add.18), channel_id=1, source_target_pairs={{0,16},{4,20},{8,24},{12,28},{16,0},{20,4},{24,8},{28,12},{1,17},{... | collective-permute-start | bytes 49160 | tf_op jit(solution)/shard_map/ppermute | solution.py:400

commit v3 on v2

--- a/solution.py
+++ b/solution.py
@@ -13,7 +13,8 @@
 INNER = (0, 1)
 SHARED = (3, 5)
 SENT = (2, 4)
-GROUP = 4
+GROUP = 8
+LEAST = 2
 ROWS = ((4, 1, 0), (3, 2))
 
 F32 = jnp.float32
@@ -42,48 +43,56 @@
     )
 
 
-def compose(faces, face_ref, class_ref, held, first_ref, last_ref, sum_ref, lists, part):
-    ids, kinds, places = lists
+def listed(face_ref, class_ref, order):
     subs, elems = face_ref.shape
-    half = held.shape[2]
-    total = jnp.int32(0)
+    front, back = jnp.int32(0), jnp.int32(subs * elems - 1)
     for s in range(subs):
         for e in range(elems):
             face = face_ref[s, e]
-            place = jnp.int32(s * len(faces))
-            hit = face == faces[0]
-            for i in range(1, len(faces)):
-                hit = hit | (face == faces[i])
-                place = jnp.where(face == faces[i], s * len(faces) + i, place)
-            ids[total] = s * elems + e
-            kinds[total] = class_ref[s, e]
-            places[total] = place
-            total = total + hit.astype(jnp.int32)
+            hit = (face == SENT[0]) | (face == SENT[1])
+            order[jnp.where(hit, front, back)] = (
+                (s * elems + e) * 4096 + (face * subs + s) * 64 + class_ref[s, e]
+            )
+            hit = hit.astype(jnp.int32)
+            front, back = front + hit, back - 1 + hit
+    return front
+
+
+def groups(count):
+    return (count + GROUP - 1) // GROUP
+
+
+def stop_of(sent):
+    return jnp.maximum(groups(sent), LEAST)
+
+
+def compose(span, total, held, first_ref, last_ref, sum_ref, order, part):
+    half = held.shape[2]
     sum_ref[...] = jnp.zeros_like(sum_ref)
 
     def group(g, carry):
-        where = [jnp.minimum(g * GROUP + u, total - 1) for u in range(GROUP)]
+        words = [order[jnp.minimum(g * GROUP + u, total - 1)] for u in range(GROUP)]
         for u in range(GROUP):
-            kind = kinds[where[u]]
-            wide = embedded(held[ids[where[u]], 0], held[ids[where[u]], 1])
+            kind = words[u] & 63
+            e = lax.shift_right_logical(words[u], 12)
+            wide = embedded(held[e, 0], held[e, 1])
             out = dot(first_ref[kind], wide, True)
             out = dot(doubled(out), wide)
-            out = dot(doubled(out[:half] + out[half:]), last_ref[kind], True)
+            out = dot(doubled(out[:half] + out[half:]), last_ref[kind])
             part[u] = out[:half] + out[half:]
         for u in range(GROUP):
-            at = places[where[u]]
+            at = lax.shift_right_logical(words[u], 6) & 63
             sum_ref[at] = sum_ref[at] + jnp.where(g * GROUP + u < total, part[u], 0.0)
         return carry
 
-    lax.fori_loop(0, (total + GROUP - 1) // GROUP, group, 0)
-
-
-def pack(out_ref, sum_ref, start_of, partner_ref, face, subs):
-    half = sum_ref.shape[1]
+    lax.fori_loop(span[0], span[1], group, 0)
+
+
+def pack(out_ref, operator_of, start_of, partner_ref, face, subs):
     for s in range(subs):
         real, imag = start_of(s)
-        rhs = real.shape[0]
-        out_ref[s, :half] = sum_ref[s]
+        rhs, half = real.shape
+        out_ref[s, :half] = operator_of(s)
         out_ref[s, half : half + rhs, :half] = real
         out_ref[s, half : half + rhs, half:] = imag
         partner = partner_ref[s, face]
@@ -93,47 +102,47 @@
         out_ref[s, half + rhs + 8 : half + rhs + 16] = jnp.full((8, 2 * half), there, F32)
 
 
-def compose_slab(face_hbm, class_hbm, partner_hbm, inv_ref, load_ref, trace_ref, start_ref,
-                 out_ref, held, first_ref, last_ref, sum_ref, part, ids, kinds, places,
-                 load, trace, rows, face_ref, class_ref, partner_ref, sems):
+def compose_sent(face_hbm, class_hbm, partner_hbm, inv_ref, load_ref, trace_ref, start_ref,
+                 to_sub, to_slab, held, first_ref, last_ref, sum_ref, part, order,
+                 load, trace, sub_rows, slab_rows, face_ref, class_ref, partner_ref, sems):
     subs = face_ref.shape[0]
     half = load_ref.shape[2]
-    pieces = sems.shape[0] - 6
-    step = inv_ref.shape[0] // pieces
-    copies = [
-        pltpu.make_async_copy(load_ref, load, sems.at[0]),
-        pltpu.make_async_copy(trace_ref, trace, sems.at[1]),
-        pltpu.make_async_copy(start_ref.at[:, SENT[1]], rows, sems.at[2]),
-    ]
-    for i, (source, place) in enumerate(
-        ((face_hbm, face_ref), (class_hbm, class_ref), (partner_hbm, partner_ref))
+    copies = []
+    for source, place in (
+        (load_ref, load),
+        (trace_ref, trace),
+        (face_hbm, face_ref),
+        (class_hbm, class_ref),
+        (start_ref.at[:, SENT[0]], sub_rows),
+        (start_ref.at[:, SENT[1]], slab_rows),
+        (partner_hbm, partner_ref),
     ):
-        copies.append(pltpu.make_async_copy(source, place, sems.at[3 + i]))
-    for i in range(pieces):
+        copies.append(pltpu.make_async_copy(source, place, sems.at[len(copies)]))
+    small = len(copies)
+    step = inv_ref.shape[0] // (sems.shape[0] - small)
+    for i in range(sems.shape[0] - small):
         span = pl.ds(i * step, step)
-        copies.append(pltpu.make_async_copy(inv_ref.at[span], held.at[span], sems.at[6 + i]))
+        copies.append(
+            pltpu.make_async_copy(inv_ref.at[span], held.at[span], sems.at[small + i])
+        )
     for copy in copies:
         copy.start()
-    copies[0].wait()
-    copies[1].wait()
+    for copy in copies[:2]:
+        copy.wait()
     for c in range(load_ref.shape[0]):
         for x in range(2):
             first_ref[c, :, x * half : (x + 1) * half] = load[c, x].astype(F32).T.astype(BF16)
-        last_ref[c] = embedded(trace[c, 0], trace[c, 1])
-    for copy in copies[2:]:
+        real, imag = [trace[c, x].astype(F32).T.astype(BF16) for x in range(2)]
+        last_ref[c] = embedded(real, -imag)
+    for copy in copies[2:small]:
         copy.wait()
-    compose(SENT[1:], face_ref, class_ref, held, first_ref, last_ref, sum_ref,
-            (ids, kinds, places), part)
-    pack(out_ref, sum_ref, lambda s: (rows[s, 0], rows[s, 1]), partner_ref, SENT[1], subs)
-
-
-def compose_sub(face_ref, class_ref, partner_ref, held, first_ref, last_ref, start_ref,
-                out_ref, sum_ref, part, ids, kinds, places):
-    subs = face_ref.shape[0]
-    compose(SENT[:1], face_ref, class_ref, held, first_ref, last_ref, sum_ref,
-            (ids, kinds, places), part)
-    pack(out_ref, sum_ref, lambda s: (start_ref[s, SENT[0], 0], start_ref[s, SENT[0], 1]),
-         partner_ref, SENT[0], subs)
+    stop = stop_of(listed(face_ref, class_ref, order))
+    for copy in copies[small:]:
+        copy.wait()
+    compose((0, stop), held.shape[0], held, first_ref, last_ref, sum_ref, order, part)
+    for out_ref, rows, face in ((to_sub, sub_rows, SENT[0]), (to_slab, slab_rows, SENT[1])):
+        pack(out_ref, lambda s: sum_ref[face * subs + s], lambda s: (rows[s, 0], rows[s, 1]),
+             partner_ref, face, subs)
 
 
 def spread(rows):
@@ -159,16 +168,18 @@
 
 
 def compose_kept(face_ref, class_ref, partner_ref, partner_face_ref, held, first_ref, last_ref,
-                 start_ref, wide_high, wide_low, rows_high, rows_low, gram_ref,
-                 sum_ref, part, ids, kinds, places, inner_high, inner_low, now_ref, out_ref):
+                 start_ref, sent_sum, wide_high, wide_low, rows_high, rows_low, gram_ref,
+                 sum_ref, part, order, inner_high, inner_low, now_ref, out_ref):
     subs, _, _, rhs, _ = start_ref.shape
     faces = INNER + SHARED
     inner = len(INNER)
-    compose(faces, face_ref, class_ref, held, first_ref, last_ref, sum_ref,
-            (ids, kinds, places), part)
+    stop = stop_of(listed(face_ref, class_ref, order))
+    total = held.shape[0]
+    compose((stop, groups(total)), total, held, first_ref, last_ref, sum_ref, order, part)
     for s in range(subs):
-        for i in range(len(faces)):
-            high, low = spread(sum_ref[s * len(faces) + i])
+        for i, face in enumerate(faces):
+            at = face * subs + s
+            high, low = spread(sent_sum[at] + sum_ref[at])
             if i < inner:
                 inner_high[s * inner + i] = high
                 inner_low[s * inner + i] = low
@@ -418,14 +429,8 @@
     def shape(*dims, dtype=F32):
         return jax.ShapeDtypeStruct(dims, dtype)
 
-    def scratch(sums):
-        return [
-            pltpu.VMEM((sums, half, full), F32),
-            pltpu.VMEM((GROUP, half, full), F32),
-            pltpu.SMEM((subs * elems + 1,), jnp.int32),
-            pltpu.SMEM((subs * elems + 1,), jnp.int32),
-            pltpu.SMEM((subs * elems + 1,), jnp.int32),
-        ]
+    sums = shape(start.shape[1] * subs, half, full)
+    scratch = [pltpu.VMEM((GROUP, half, full), F32), pltpu.SMEM((subs * elems,), jnp.int32)]
 
     def call(kernel, out_shape, in_specs, scratch_shapes):
         return pl.pallas_call(
@@ -449,26 +454,23 @@
         pltpu.with_memory_space_constraint(x, pltpu.HBM)
         for x in (elem_face, elem_class, partner, inv_factor, load_map, trace_map, start)
     ]
-    to_slab, held, first, last = call(
-        compose_slab,
-        (load, shape(*inv_factor.shape, dtype=BF16), shape(classes, half, full, dtype=BF16),
-         shape(classes, full, full, dtype=BF16)),
+    to_sub, to_slab, held, first, last, sent_sum = call(
+        compose_sent,
+        (load, load, shape(*inv_factor.shape, dtype=BF16), shape(classes, half, full, dtype=BF16),
+         shape(classes, full, full, dtype=BF16), sums),
         [hbm] * 7,
-        scratch(subs) + [
+        scratch + [
             pltpu.VMEM(load_map.shape, BF16),
             pltpu.VMEM(trace_map.shape, BF16),
+            pltpu.VMEM((subs, 2, rhs, half), F32),
             pltpu.VMEM((subs, 2, rhs, half), F32),
             pltpu.SMEM(elem_face.shape, jnp.int32),
             pltpu.SMEM(elem_class.shape, jnp.int32),
             pltpu.SMEM(partner.shape, jnp.int32),
-            pltpu.SemaphoreType.DMA((6 + 4,)),
+            pltpu.SemaphoreType.DMA((7 + 4,)),
         ],
     )(*far)
     from_slab = shifted(to_slab, "slab", False)
-
-    (to_sub,) = call(
-        compose_sub, (load,), [smem, smem, smem] + [vmem] * 4, scratch(subs)
-    )(elem_face, elem_class, partner, held, first, last, start)
     from_sub = shifted(to_sub, "sub", False)
 
     slots = 2 * subs
@@ -477,14 +479,14 @@
     wide_high, wide_low, inner_high, inner_low, inner_gram = call(
         compose_kept,
         (square, square, rows, rows, shape(size, 128)),
-        [smem, smem, smem, smem] + [vmem] * 4,
-        scratch(2 * slots) + [
+        [smem, smem, smem, smem] + [vmem] * 5,
+        [pltpu.VMEM(sums.shape, F32)] + scratch + [
             pltpu.VMEM((slots, full, full), BF16),
             pltpu.VMEM((slots, full, full), BF16),
             pltpu.VMEM((slots, rhs, full), F32),
             pltpu.VMEM((slots, rhs, full), F32),
         ],
-    )(elem_face, elem_class, partner, partner_face, held, first, last, start)
+    )(elem_face, elem_class, partner, partner_face, held, first, last, start, sent_sum)
 
     back = shape(subs, ITERS * rhs, full)
     gram, rows_high, rows_low, ret_sub, ret_slab = call(

time: 53.5 us -> 53.3 us (level)
  waiting for transfers between devices: 15.2 us -> 17.9 us
  Pallas kernels: 20.5 us -> 19 us
  starting transfers between devices: 16.7 us -> 15.3 us
    pallas_call x1, Pallas kernels: 6.36 us -> 4.43 us  [body(): call(compose_kept, (square, square, rows, rows, shape(size, 128)), [smem,...]
    ppermute x4, waiting for transfers between devices: 4.64 us -> 6.53 us  [shifted(): lax.ppermute(x, axis, [(i, i + 1) if up else (i + 1, i) for i in range(la...]
    ppermute x5, starting transfers between devices: 8.79 us -> 6.91 us  [summed(): received.append(lax.ppermute(x, axis, pairs))]
    ppermute x5, waiting for transfers between devices: 10.6 us -> 11.4 us  [summed(): received.append(lax.ppermute(x, axis, pairs))]
    pallas_call x2 -> x1, Pallas kernels: 7.7 us -> 8.17 us  [body(): call(compose_sent, (load, load, shape(*inv_factor.shape, dtype=BF16), sha...]
  transfers between devices with their start and end apart: 9 -> 9, of which waited for: 6 -> 6; matrix products, arithmetic and copies ran while one was open for 0% -> 0% of each run, Pallas kernels for 12% -> 8%
where the time goes in v3:
time: 53.3 us; the launch traced here: 53.1 us
  Pallas kernels  19 us (36%)
  waiting for transfers between devices  17.9 us (34%)
  starting transfers between devices  15.3 us (29%)
  between operations  0.79 us (1%)
    ppermute x5, waiting for transfers between devices, summed(): received.append(lax.ppermute(x, axis, pairs))  11.4 us
    ppermute x4, starting transfers between devices, shifted(): lax.ppermute(x, axis, [(i, i + 1) if up else (i + 1, i) for i in range(la...  8.37 us
    pallas_call x1, Pallas kernels, body(): call(compose_sent, (load, load, shape(*inv_factor.shape, dtype=BF16), sha...  8.17 us
    ppermute x5, starting transfers between devices, summed(): received.append(lax.ppermute(x, axis, pairs))  6.91 us
    ppermute x4, waiting for transfers between devices, shifted(): lax.ppermute(x, axis, [(i, i + 1) if up else (i + 1, i) for i in range(la...  6.53 us
    pallas_call x1, Pallas kernels, body(): call(compose_kept, (square, square, rows, rows, shape(size, 128)), [smem,...  4.43 us
    pallas_call x1, Pallas kernels, body(): call(functools.partial(finish, float(count)), (shape(*start.shape), shape...  3.98 us
    pallas_call x1, Pallas kernels, body(): call(krylov, (shape(2 * rhs, 128), rows, rows, back, back), [smem] + [vme...  2.45 us
  transfers between devices with their start and end apart: 9, of which 6 were waited for; matrix products, arithmetic and copies ran while one was open for 0% of the time, Pallas kernels for 8%

profile of v3, /device:TPU:0, one launch (start us, length us, event | category | flops | bytes accessed | tf_op | source)
XLA Modules:
  0.0 53.1 jit_solution(15133159583502387367)
XLA Ops:
  0.6 0.0 copy-start
  0.6 0.0 copy-start.4
  0.7 8.2 %shard_map.95 = (f32[2,160,256]{2,1,0:T(8,128)S(1)}, f32[2,160,256]{2,1,0:T(8,128)S(1)}, bf16[32,2,128,128]{3,2,1,0:T(8,128)(2,1)S(1)}, bf16[4,128,256]{2,1,0:T(...) custom-call(s32[2,16]{1,0:T(2,128)} %face_ref.1, s32[2,16]{1,0:T(2,128)} %class_ref.1, ...), custom_call_target="tpu_custom_call" | custom-call | flops 2000000000 | bytes 4000000 | tf_op jit(solution)/shard_map/pallas_call | solution.py:457
  8.9 1.3 %collective-permute-start = (f32[2,160,256]{2,1,0:T(8,128)S(1)}, f32[2,160,256]{2,1,0:T(8,128)S(1)}, u32[]{:S(2)}, u32[]{:S(2)}) collective-permute-start(f32[2,160,256]{2,1,0:T(8,128)S(1)} %get-tuple-element.24), channel_id=1, source_target_pairs={{1,0},{2,1},{3,2},{5,4},{6,5},{7,6},{9,8},{10,9},{11,10},{13,12},{... | collective-permute-start | bytes 983048 | tf_op jit(solution)/shard_map/ppermute | solution.py:450
  10.2 1.3 %collective-permute-start.1 = (f32[2,160,256]{2,1,0:T(8,128)S(1)}, f32[2,160,256]{2,1,0:T(8,128)S(1)}, u32[]{:S(2)}, u32[]{:S(2)}) collective-permute-start(f32[2,160,256]{2,1,0:T(8,128)S(1)} %get-tuple-element.25), channel_id=1, source_target_pairs={{4,0},{8,4},{12,8},{16,12},{20,16},{24,20},{28,24},{5,1},{9,5},{13... | collective-permute-start | bytes 983048 | tf_op jit(solution)/shard_map/ppermute | solution.py:450
  11.5 4.4 %shard_map.96 = (bf16[4,256,256]{2,1,0:T(8,128)(2,1)S(1)}, bf16[4,256,256]{2,1,0:T(8,128)(2,1)S(1)}, bf16[4,80,256]{2,1,0:T(8,128)(2,1)S(1)}, bf16[4,80,256]{2,1,0:T(8,128)(2,1)S(1)}, f32[80,128]{1,0:T(8,128)S(1)}) custom-call(s32[2,16]{1,0:T(2,128)S(1)} %copy-done.1, s32[2,16]{1,0:T(2,128)S(1)} %copy-done.2, s32[2,6]{1,0:T(2,128)S(1)} %copy-done.4, ...), custom_call_target="tpu_custom_call" | custom-call | flops 2000000000 | bytes 4000000 | tf_op jit(solution)/shard_map/pallas_call | solution.py:479
  15.9 0.0 collective-permute-done.from_sub_ref
  16.0 6.5 %collective-permute-done.1.from_slab_ref = f32[2,160,256]{2,1,0:T(8,128)S(1)} collective-permute-done((f32[2,160,256]{2,1,0:T(8,128)S(1)}, f32[2,160,256]{2,1,0:T(8,128)S(1)}, u32[]{:S(2)}, u32[]{:S(2)}) %collective-permute-start.1) | collective-permute-done | bytes 327712 | tf_op jit(solution)/shard_map/ppermute | solution.py:450
  22.5 2.5 %shard_map.97 = (f32[32,128]{1,0:T(8,128)S(1)}, bf16[4,80,256]{2,1,0:T(8,128)(2,1)S(1)}, bf16[4,80,256]{2,1,0:T(8,128)(2,1)S(1)}, f32[2,64,256]{2,1,0:T(8,128)S(1)}, f32[2,64,256]{2,1,0:T(8,128)S(1)}) custom-call(s32[2,6]{1,0:T(2,128)S(1)} %copy-done.4, bf16[4,256,256]{2,1,0:T(8,128)(2,1)S(1)} %get-tuple-element.22.wide_high, ...), custom_call_target="tpu_custom_call" | custom-call | flops 2000000000 | bytes 4000000 | tf_op jit(solution)/shard_map/pallas_call | solution.py:492
  24.9 2.0 %collective-permute-start.7 = (f32[2,64,256]{2,1,0:T(8,128)S(1)}, f32[2,64,256]{2,1,0:T(8,128)S(1)}, u32[]{:S(2)}, u32[]{:S(2)}) collective-permute-start(f32[2,64,256]{2,1,0:T(8,128)S(1)} %get-tuple-element.32), channel_id=1, source_target_pairs={{0,1},{1,2},{2,3},{4,5},{5,6},{6,7},{8,9},{9,10},{10,11},{12,13},{... | collective-permute-start | bytes 393224 | tf_op jit(solution)/shard_map/ppermute | solution.py:450
  27.0 3.8 %collective-permute-start.8 = (f32[2,64,256]{2,1,0:T(8,128)S(1)}, f32[2,64,256]{2,1,0:T(8,128)S(1)}, u32[]{:S(2)}, u32[]{:S(2)}) collective-permute-start(f32[2,64,256]{2,1,0:T(8,128)S(1)} %get-tuple-element.33), channel_id=1, source_target_pairs={{0,4},{4,8},{8,12},{12,16},{16,20},{20,24},{24,28},{1,5},{5,9},{9,... | collective-permute-start | bytes 393224 | tf_op jit(solution)/shard_map/ppermute | solution.py:450
  30.7 1.6 %collective-permute-start.2 = (f32[32,128]{1,0:T(8,128)S(1)}, f32[32,128]{1,0:T(8,128)S(1)}, u32[]{:S(2)}, u32[]{:S(2)}) collective-permute-start(f32[32,128]{1,0:T(8,128)S(1)} %get-tuple-element.27), channel_id=1, source_target_pairs={{0,1},{1,0},{2,3},{3,2},{4,5},{5,4},{6,7},{7,6},{8,9},{9,8},{10,11... | collective-permute-start | bytes 49160 | tf_op jit(solution)/shard_map/ppermute | solution.py:411
  32.3 0.8 %collective-permute-done.2 = f32[32,128]{1,0:T(8,128)S(1)} collective-permute-done((f32[32,128]{1,0:T(8,128)S(1)}, f32[32,128]{1,0:T(8,128)S(1)}, u32[]{:S(2)}, u32[]{:S(2)}) %collective-permute-start.2) | collective-permute-done | bytes 16416 | tf_op jit(solution)/shard_map/ppermute | solution.py:411
  33.2 0.5 collective-permute-start.3
  33.7 3.2 %collective-permute-done.3 = f32[32,128]{1,0:T(8,128)S(1)} collective-permute-done((f32[32,128]{1,0:T(8,128)S(1)}, f32[32,128]{1,0:T(8,128)S(1)}, u32[]{:S(2)}, u32[]{:S(2)}) %collective-permute-start.3) | collective-permute-done | bytes 16416 | tf_op jit(solution)/shard_map/ppermute | solution.py:411
  36.9 0.6 %collective-permute-start.4 = (f32[32,128]{1,0:T(8,128)S(1)}, f32[32,128]{1,0:T(8,128)S(1)}, u32[]{:S(2)}, u32[]{:S(2)}) collective-permute-start(f32[32,128]{1,0:T(8,128)S(1)} %add.16), channel_id=1, source_target_pairs={{0,4},{4,0},{8,12},{12,8},{16,20},{20,16},{24,28},{28,24},{1,5},{5... | collective-permute-start | bytes 49160 | tf_op jit(solution)/shard_map/ppermute | solution.py:411
  37.5 3.1 %collective-permute-done.4 = f32[32,128]{1,0:T(8,128)S(1)} collective-permute-done((f32[32,128]{1,0:T(8,128)S(1)}, f32[32,128]{1,0:T(8,128)S(1)}, u32[]{:S(2)}, u32[]{:S(2)}) %collective-permute-start.4) | collective-permute-done | bytes 16416 | tf_op jit(solution)/shard_map/ppermute | solution.py:411
  40.7 1.6 %collective-permute-start.5 = (f32[32,128]{1,0:T(8,128)S(1)}, f32[32,128]{1,0:T(8,128)S(1)}, u32[]{:S(2)}, u32[]{:S(2)}) collective-permute-start(f32[32,128]{1,0:T(8,128)S(1)} %add.17), channel_id=1, source_target_pairs={{0,8},{4,12},{8,0},{12,4},{16,24},{20,28},{24,16},{28,20},{1,9},{5... | collective-permute-start | bytes 49160 | tf_op jit(solution)/shard_map/ppermute | solution.py:411
  42.3 2.2 %collective-permute-done.5 = f32[32,128]{1,0:T(8,128)S(1)} collective-permute-done((f32[32,128]{1,0:T(8,128)S(1)}, f32[32,128]{1,0:T(8,128)S(1)}, u32[]{:S(2)}, u32[]{:S(2)}) %collective-permute-start.5) | collective-permute-done | bytes 16416 | tf_op jit(solution)/shard_map/ppermute | solution.py:411
  44.4 2.6 %collective-permute-start.6 = (f32[32,128]{1,0:T(8,128)S(1)}, f32[32,128]{1,0:T(8,128)S(1)}, u32[]{:S(2)}, u32[]{:S(2)}) collective-permute-start(f32[32,128]{1,0:T(8,128)S(1)} %add.18), channel_id=1, source_target_pairs={{0,16},{4,20},{8,24},{12,28},{16,0},{20,4},{24,8},{28,12},{1,17},{... | collective-permute-start | bytes 49160 | tf_op jit(solution)/shard_map/ppermute | solution.py:411
  47.0 2.0 %collective-permute-done.6 = f32[32,128]{1,0:T(8,128)S(1)} collective-permute-done((f32[32,128]{1,0:T(8,128)S(1)}, f32[32,128]{1,0:T(8,128)S(1)}, u32[]{:S(2)}, u32[]{:S(2)}) %collective-permute-start.6) | collective-permute-done | bytes 16416 | tf_op jit(solution)/shard_map/ppermute | solution.py:411
  49.1 0.0 collective-permute-done.7.back_sub_ref
  49.1 0.0 collective-permute-done.8.back_slab_ref
  49.1 4.0 %shard_map.98 = (f32[2,6,2,16,128]{4,3,2,1,0:T(8,128)}, f32[4,5,16,16]{3,2,1,0:T(8,128)}) custom-call(f32[32,128]{1,0:T(8,128)S(1)} %add.19.gram_ref, bf16[4,80,256]{2,1,0:T(8,128)(2,1)S(1)} %get-tuple-element.28.inner_high, bf16[4,80,256]{2,1,0:T(8,128)(2,1)S(1)} %get-tuple-element.29.inner_low, bf16[4,80,256]{2,1,0:T(8,128)(2,1)S(1)} %get-tuple-element.30.rows_high, ...), custom_call_target="tpu_custom_call" | custom-call | flops 2000000000 | bytes 4000000 | tf_op jit(solution)/shard_map/pallas_call | solution.py:510
  (13 shorter events, 0.0 us)
Async XLA Ops:
  0.6 10.8 %copy-start = (f32[2,6,2,16,128]{4,3,2,1,0:T(8,128)S(1)}, f32[2,6,2,16,128]{4,3,2,1,0:T(8,128)}, u32[]{:S(2)}) copy-start(f32[2,6,2,16,128]{4,3,2,1,0:T(8,128)} %start_ref.7) | copy-start | bytes 589828
  0.6 10.8 %copy-start.4 = (s32[2,6]{1,0:T(2,128)S(1)}, s32[2,6]{1,0:T(2,128)}, u32[]{:S(2)}) copy-start(s32[2,6]{1,0:T(2,128)} %partner_ref.3) | copy-start | bytes 148
  0.7 10.8 %copy-start.1 = (s32[2,16]{1,0:T(2,128)S(1)}, s32[2,16]{1,0:T(2,128)}, u32[]{:S(2)}) copy-start(s32[2,16]{1,0:T(2,128)} %face_ref.1) | copy-start | bytes 388
  0.7 10.8 %copy-start.2 = (s32[2,16]{1,0:T(2,128)S(1)}, s32[2,16]{1,0:T(2,128)}, u32[]{:S(2)}) copy-start(s32[2,16]{1,0:T(2,128)} %class_ref.1) | copy-start | bytes 388
  0.7 10.8 %copy-start.3 = (s32[2,6]{1,0:T(2,128)S(1)}, s32[2,6]{1,0:T(2,128)}, u32[]{:S(2)}) copy-start(s32[2,6]{1,0:T(2,128)} %partner_face_ref.1) | copy-start | bytes 148
  8.9 7.1 %collective-permute-start = (f32[2,160,256]{2,1,0:T(8,128)S(1)}, f32[2,160,256]{2,1,0:T(8,128)S(1)}, u32[]{:S(2)}, u32[]{:S(2)}) collective-permute-start(f32[2,160,256]{2,1,0:T(8,128)S(1)} %get-tuple-element.24), channel_id=1, source_target_pairs={{1,0},{2,1},{3,2},{5,4},{6,5},{7,6},{9,8},{10,9},{11,10},{13,12},{... | collective-permute-start | bytes 983048 | tf_op jit(solution)/shard_map/ppermute | solution.py:450
  10.2 12.3 %collective-permute-start.1 = (f32[2,160,256]{2,1,0:T(8,128)S(1)}, f32[2,160,256]{2,1,0:T(8,128)S(1)}, u32[]{:S(2)}, u32[]{:S(2)}) collective-permute-start(f32[2,160,256]{2,1,0:T(8,128)S(1)} %get-tuple-element.25), channel_id=1, source_target_pairs={{4,0},{8,4},{12,8},{16,12},{20,16},{24,20},{28,24},{5,1},{9,5},{13... | collective-permute-start | bytes 983048 | tf_op jit(solution)/shard_map/ppermute | solution.py:450
  24.9 24.1 %collective-permute-start.7 = (f32[2,64,256]{2,1,0:T(8,128)S(1)}, f32[2,64,256]{2,1,0:T(8,128)S(1)}, u32[]{:S(2)}, u32[]{:S(2)}) collective-permute-start(f32[2,64,256]{2,1,0:T(8,128)S(1)} %get-tuple-element.32), channel_id=1, source_target_pairs={{0,1},{1,2},{2,3},{4,5},{5,6},{6,7},{8,9},{9,10},{10,11},{12,13},{... | collective-permute-start | bytes 393224 | tf_op jit(solution)/shard_map/ppermute | solution.py:450
  27.0 22.1 %collective-permute-start.8 = (f32[2,64,256]{2,1,0:T(8,128)S(1)}, f32[2,64,256]{2,1,0:T(8,128)S(1)}, u32[]{:S(2)}, u32[]{:S(2)}) collective-permute-start(f32[2,64,256]{2,1,0:T(8,128)S(1)} %get-tuple-element.33), channel_id=1, source_target_pairs={{0,4},{4,8},{8,12},{12,16},{16,20},{20,24},{24,28},{1,5},{5,9},{9,... | collective-permute-start | bytes 393224 | tf_op jit(solution)/shard_map/ppermute | solution.py:450
  30.7 2.4 %collective-permute-start.2 = (f32[32,128]{1,0:T(8,128)S(1)}, f32[32,128]{1,0:T(8,128)S(1)}, u32[]{:S(2)}, u32[]{:S(2)}) collective-permute-start(f32[32,128]{1,0:T(8,128)S(1)} %get-tuple-element.27), channel_id=1, source_target_pairs={{0,1},{1,0},{2,3},{3,2},{4,5},{5,4},{6,7},{7,6},{8,9},{9,8},{10,11... | collective-permute-start | bytes 49160 | tf_op jit(solution)/shard_map/ppermute | solution.py:411
  33.2 3.7 %collective-permute-start.3 = (f32[32,128]{1,0:T(8,128)S(1)}, f32[32,128]{1,0:T(8,128)S(1)}, u32[]{:S(2)}, u32[]{:S(2)}) collective-permute-start(f32[32,128]{1,0:T(8,128)S(1)} %add.15), channel_id=1, source_target_pairs={{0,2},{1,3},{2,0},{3,1},{4,6},{5,7},{6,4},{7,5},{8,10},{9,11},{10,... | collective-permute-start | bytes 49160 | tf_op jit(solution)/shard_map/ppermute | solution.py:411
  36.9 3.7 %collective-permute-start.4 = (f32[32,128]{1,0:T(8,128)S(1)}, f32[32,128]{1,0:T(8,128)S(1)}, u32[]{:S(2)}, u32[]{:S(2)}) collective-permute-start(f32[32,128]{1,0:T(8,128)S(1)} %add.16), channel_id=1, source_target_pairs={{0,4},{4,0},{8,12},{12,8},{16,20},{20,16},{24,28},{28,24},{1,5},{5... | collective-permute-start | bytes 49160 | tf_op jit(solution)/shard_map/ppermute | solution.py:411
  40.7 3.7 %collective-permute-start.5 = (f32[32,128]{1,0:T(8,128)S(1)}, f32[32,128]{1,0:T(8,128)S(1)}, u32[]{:S(2)}, u32[]{:S(2)}) collective-permute-start(f32[32,128]{1,0:T(8,128)S(1)} %add.17), channel_id=1, source_target_pairs={{0,8},{4,12},{8,0},{12,4},{16,24},{20,28},{24,16},{28,20},{1,9},{5... | collective-permute-start | bytes 49160 | tf_op jit(solution)/shard_map/ppermute | solution.py:411
  44.4 4.6 %collective-permute-start.6 = (f32[32,128]{1,0:T(8,128)S(1)}, f32[32,128]{1,0:T(8,128)S(1)}, u32[]{:S(2)}, u32[]{:S(2)}) collective-permute-start(f32[32,128]{1,0:T(8,128)S(1)} %add.18), channel_id=1, source_target_pairs={{0,16},{4,20},{8,24},{12,28},{16,0},{20,4},{24,8},{28,12},{1,17},{... | collective-permute-start | bytes 49160 | tf_op jit(solution)/shard_map/ppermute | solution.py:411

commit v4 on v3

--- a/solution.py
+++ b/solution.py
@@ -31,10 +31,6 @@
 def two_parts(x):
     high = x.astype(BF16)
     return high, (x - high.astype(F32)).astype(BF16)
-
-
-def doubled(x):
-    return jnp.concatenate(two_parts(x), axis=0)
 
 
 def embedded(real, imag):
@@ -67,7 +63,6 @@
 
 
 def compose(span, total, held, first_ref, last_ref, sum_ref, order, part):
-    half = held.shape[2]
     sum_ref[...] = jnp.zeros_like(sum_ref)
 
     def group(g, carry):
@@ -77,9 +72,8 @@
             e = lax.shift_right_logical(words[u], 12)
             wide = embedded(held[e, 0], held[e, 1])
             out = dot(first_ref[kind], wide, True)
-            out = dot(doubled(out), wide)
-            out = dot(doubled(out[:half] + out[half:]), last_ref[kind])
-            part[u] = out[:half] + out[half:]
+            out = dot(out.astype(BF16), wide)
+            part[u] = dot(out.astype(BF16), last_ref[kind])
         for u in range(GROUP):
             at = lax.shift_right_logical(words[u], 6) & 63
             sum_ref[at] = sum_ref[at] + jnp.where(g * GROUP + u < total, part[u], 0.0)
@@ -148,13 +142,13 @@
 def spread(rows):
     half = rows.shape[0]
     lower = jnp.concatenate([-rows[:, half:], rows[:, :half]], axis=1)
-    return two_parts(jnp.concatenate([rows, lower], axis=0))
-
-
-def leaving(high, low, x, wide_high, wide_low):
+    return jnp.concatenate([rows, lower], axis=0).astype(BF16)
+
+
+def leaving(high, low, x, wide):
     rhs = x.shape[0]
-    both = dot(jnp.concatenate([high, low], axis=0), wide_high)
-    return (both[:rhs] + both[rhs:] + dot(high, wide_low) - x) * STEP_SCALE
+    both = dot(jnp.concatenate([high, low], axis=0), wide)
+    return (both[:rhs] + both[rhs:] - x) * STEP_SCALE
 
 
 def products(pairs):
@@ -168,8 +162,8 @@
 
 
 def compose_kept(face_ref, class_ref, partner_ref, partner_face_ref, held, first_ref, last_ref,
-                 start_ref, sent_sum, wide_high, wide_low, rows_high, rows_low, gram_ref,
-                 sum_ref, part, order, inner_high, inner_low, now_ref, out_ref):
+                 start_ref, sent_sum, wide_ref, rows_high, rows_low, gram_ref,
+                 sum_ref, part, order, inner_wide, now_ref, out_ref):
     subs, _, _, rhs, _ = start_ref.shape
     faces = INNER + SHARED
     inner = len(INNER)
@@ -179,14 +173,11 @@
     for s in range(subs):
         for i, face in enumerate(faces):
             at = face * subs + s
-            high, low = spread(sent_sum[at] + sum_ref[at])
+            wide = spread(sent_sum[at] + sum_ref[at])
             if i < inner:
-                inner_high[s * inner + i] = high
-                inner_low[s * inner + i] = low
+                inner_wide[s * inner + i] = wide
             else:
-                at = (i - inner) * subs + s
-                wide_high[at] = high
-                wide_low[at] = low
+                wide_ref[(i - inner) * subs + s] = wide
     slots = subs * inner
     for s in range(subs):
         for f in INNER:
@@ -200,7 +191,7 @@
         later = slice((k + 1) * rhs, (k + 2) * rhs)
         for at in range(slots):
             out_ref[at] = leaving(rows_high[at, now], rows_low[at, now], now_ref[at],
-                                  inner_high[at], inner_low[at])
+                                  inner_wide[at])
         for s in range(subs):
             for f in INNER:
                 local = partner_ref[s, f] % subs * inner + partner_face_ref[s, f]
@@ -215,9 +206,9 @@
     gram_ref[:, :size] = products([(rows_high[at], rows_low[at]) for at in range(slots)])
 
 
-def krylov(partner_ref, wide_high, wide_low, from_sub_ref, from_slab_ref, start_ref, inner_ref,
+def krylov(partner_ref, wide_ref, from_sub_ref, from_slab_ref, start_ref, inner_ref,
            gram_ref, rows_high, rows_low, to_sub_ref, to_slab_ref,
-           far_wide_high, far_wide_low, far_high, far_low, now_ref, out_ref):
+           far_wide, far_high, far_low, now_ref, out_ref):
     subs, _, _, rhs, half = start_ref.shape
     own = 2 * subs
     sources = (from_sub_ref, from_slab_ref)
@@ -227,7 +218,7 @@
         for s in range(subs):
             at = d * subs + s
             face = SHARED[d]
-            far_wide_high[at], far_wide_low[at] = spread(sources[d][s, :half])
+            far_wide[at] = spread(sources[d][s, :half])
             value = jnp.concatenate([start_ref[s, face, 0], start_ref[s, face, 1]], axis=1)
             now_ref[at] = value
             rows_high[at, :rhs], rows_low[at, :rhs] = two_parts(value)
@@ -240,9 +231,9 @@
         later = slice((k + 1) * rhs, (k + 2) * rhs)
         for at in range(own):
             out_ref[at] = leaving(rows_high[at, now], rows_low[at, now], now_ref[at],
-                                  wide_high[at], wide_low[at])
+                                  wide_ref[at])
             out_ref[own + at] = leaving(far_high[at, now], far_low[at, now], now_ref[own + at],
-                                        far_wide_high[at], far_wide_low[at])
+                                        far_wide[at])
         for d in range(2):
             for s in range(subs):
                 at = d * subs + s
@@ -476,12 +467,11 @@
     slots = 2 * subs
     square = shape(slots, full, full, dtype=BF16)
     rows = shape(slots, size, full, dtype=BF16)
-    wide_high, wide_low, inner_high, inner_low, inner_gram = call(
+    wide, inner_high, inner_low, inner_gram = call(
         compose_kept,
-        (square, square, rows, rows, shape(size, 128)),
+        (square, rows, rows, shape(size, 128)),
         [smem, smem, smem, smem] + [vmem] * 5,
         [pltpu.VMEM(sums.shape, F32)] + scratch + [
-            pltpu.VMEM((slots, full, full), BF16),
             pltpu.VMEM((slots, full, full), BF16),
             pltpu.VMEM((slots, rhs, full), F32),
             pltpu.VMEM((slots, rhs, full), F32),
@@ -492,16 +482,15 @@
     gram, rows_high, rows_low, ret_sub, ret_slab = call(
         krylov,
         (shape(2 * rhs, 128), rows, rows, back, back),
-        [smem] + [vmem] * 6,
+        [smem] + [vmem] * 5,
         [
-            pltpu.VMEM((slots, full, full), BF16),
             pltpu.VMEM((slots, full, full), BF16),
             pltpu.VMEM((slots, size, full), BF16),
             pltpu.VMEM((slots, size, full), BF16),
             pltpu.VMEM((2 * slots, rhs, full), F32),
             pltpu.VMEM((2 * slots, rhs, full), F32),
         ],
-    )(partner, wide_high, wide_low, from_sub, from_slab, start, inner_gram)
+    )(partner, wide, from_sub, from_slab, start, inner_gram)
 
     back_slab = shifted(ret_slab, "slab", True)
     back_sub = shifted(ret_sub, "sub", True)

time: 53.3 us -> 51.9 us (0.974)
  Pallas kernels: 19 us -> 16.3 us
  waiting for transfers between devices: 17.9 us -> 18.8 us
    pallas_call x1, Pallas kernels: 8.17 us -> 6.86 us  [body(): call(compose_sent, (load, load, shape(*inv_factor.shape, dtype=BF16), sha...]
    pallas_call x1, Pallas kernels: 4.43 us -> 3.57 us  [body(): call(compose_kept, (square, rows, rows, shape(size, 128)), [smem, smem, s...]
    ppermute x4, waiting for transfers between devices: 6.53 us -> 7.39 us  [shifted(): lax.ppermute(x, axis, [(i, i + 1) if up else (i + 1, i) for i in range(la...]
    pallas_call x1, Pallas kernels: 2.45 us -> 1.9 us  [body(): call(krylov, (shape(2 * rhs, 128), rows, rows, back, back), [smem] + [vme...]
  transfers between devices with their start and end apart: 9 -> 9, of which waited for: 6 -> 6; matrix products, arithmetic and copies ran while one was open for 0% -> 0% of each run, Pallas kernels for 8% -> 7%
where the time goes in v4:
time: 51.9 us; the launch traced here: 51.6 us
  waiting for transfers between devices  18.8 us (36%)
  Pallas kernels  16.3 us (31%)
  starting transfers between devices  15.7 us (30%)
  between operations  0.79 us (2%)
    ppermute x5, waiting for transfers between devices, summed(): received.append(lax.ppermute(x, axis, pairs))  11.4 us
    ppermute x4, starting transfers between devices, shifted(): lax.ppermute(x, axis, [(i, i + 1) if up else (i + 1, i) for i in range(la...  8.8 us
    ppermute x4, waiting for transfers between devices, shifted(): lax.ppermute(x, axis, [(i, i + 1) if up else (i + 1, i) for i in range(la...  7.39 us
    ppermute x5, starting transfers between devices, summed(): received.append(lax.ppermute(x, axis, pairs))  6.9 us
    pallas_call x1, Pallas kernels, body(): call(compose_sent, (load, load, shape(*inv_factor.shape, dtype=BF16), sha...  6.86 us
    pallas_call x1, Pallas kernels, body(): call(functools.partial(finish, float(count)), (shape(*start.shape), shape...  3.99 us
    pallas_call x1, Pallas kernels, body(): call(compose_kept, (square, rows, rows, shape(size, 128)), [smem, smem, s...  3.57 us
    pallas_call x1, Pallas kernels, body(): call(krylov, (shape(2 * rhs, 128), rows, rows, back, back), [smem] + [vme...  1.9 us
  transfers between devices with their start and end apart: 9, of which 6 were waited for; matrix products, arithmetic and copies ran while one was open for 0% of the time, Pallas kernels for 7%

profile of v4, /device:TPU:0, one launch (start us, length us, event | category | flops | bytes accessed | tf_op | source)
XLA Modules:
  0.0 51.6 jit_solution(8735417790908557289)
XLA Ops:
  0.6 0.0 copy-start
  0.6 0.0 copy-start.4
  0.7 6.9 %shard_map.95 = (f32[2,160,256]{2,1,0:T(8,128)S(1)}, f32[2,160,256]{2,1,0:T(8,128)S(1)}, bf16[32,2,128,128]{3,2,1,0:T(8,128)(2,1)S(1)}, bf16[4,128,256]{2,1,0:T(...) custom-call(s32[2,16]{1,0:T(2,128)} %face_ref.1, s32[2,16]{1,0:T(2,128)} %class_ref.1, ...), custom_call_target="tpu_custom_call" | custom-call | flops 2000000000 | bytes 4000000 | tf_op jit(solution)/shard_map/pallas_call | solution.py:448
  7.6 1.3 %collective-permute-start = (f32[2,160,256]{2,1,0:T(8,128)S(1)}, f32[2,160,256]{2,1,0:T(8,128)S(1)}, u32[]{:S(2)}, u32[]{:S(2)}) collective-permute-start(f32[2,160,256]{2,1,0:T(8,128)S(1)} %get-tuple-element.22), channel_id=1, source_target_pairs={{1,0},{2,1},{3,2},{5,4},{6,5},{7,6},{9,8},{10,9},{11,10},{13,12},{... | collective-permute-start | bytes 983048 | tf_op jit(solution)/shard_map/ppermute | solution.py:441
  8.9 1.3 %collective-permute-start.1 = (f32[2,160,256]{2,1,0:T(8,128)S(1)}, f32[2,160,256]{2,1,0:T(8,128)S(1)}, u32[]{:S(2)}, u32[]{:S(2)}) collective-permute-start(f32[2,160,256]{2,1,0:T(8,128)S(1)} %get-tuple-element.23), channel_id=1, source_target_pairs={{4,0},{8,4},{12,8},{16,12},{20,16},{24,20},{28,24},{5,1},{9,5},{13... | collective-permute-start | bytes 983048 | tf_op jit(solution)/shard_map/ppermute | solution.py:441
  10.2 3.6 %shard_map.96 = (bf16[4,256,256]{2,1,0:T(8,128)(2,1)S(1)}, bf16[4,80,256]{2,1,0:T(8,128)(2,1)S(1)}, bf16[4,80,256]{2,1,0:T(8,128)(2,1)S(1)}, f32[80,128]{1,0:T(8,128)S(1)}) custom-call(s32[2,16]{1,0:T(2,128)S(1)} %copy-done.1, s32[2,16]{1,0:T(2,128)S(1)} %copy-done.2, s32[2,6]{1,0:T(2,128)S(1)} %copy-done.4, s32[2,6]{1,0:T(2,128)S(1)} %copy-done.3, ...), custom_call_target="tpu_custom_call" | custom-call | flops 2000000000 | bytes 4000000 | tf_op jit(solution)/shard_map/pallas_call | solution.py:470
  13.8 0.0 collective-permute-done.from_sub_ref
  13.8 7.4 %collective-permute-done.1.from_slab_ref = f32[2,160,256]{2,1,0:T(8,128)S(1)} collective-permute-done((f32[2,160,256]{2,1,0:T(8,128)S(1)}, f32[2,160,256]{2,1,0:T(8,128)S(1)}, u32[]{:S(2)}, u32[]{:S(2)}) %collective-permute-start.1) | collective-permute-done | bytes 327712 | tf_op jit(solution)/shard_map/ppermute | solution.py:441
  21.2 1.9 %shard_map.97 = (f32[32,128]{1,0:T(8,128)S(1)}, bf16[4,80,256]{2,1,0:T(8,128)(2,1)S(1)}, bf16[4,80,256]{2,1,0:T(8,128)(2,1)S(1)}, f32[2,64,256]{2,1,0:T(8,128)S(1)}, f32[2,64,256]{2,1,0:T(8,128)S(1)}) custom-call(s32[2,6]{1,0:T(2,128)S(1)} %copy-done.4, bf16[4,256,256]{2,1,0:T(8,128)(2,1)S(1)} %get-tuple-element.21.wide_ref, ...), custom_call_target="tpu_custom_call" | custom-call | flops 2000000000 | bytes 4000000 | tf_op jit(solution)/shard_map/pallas_call | solution.py:482
  23.1 2.0 %collective-permute-start.7 = (f32[2,64,256]{2,1,0:T(8,128)S(1)}, f32[2,64,256]{2,1,0:T(8,128)S(1)}, u32[]{:S(2)}, u32[]{:S(2)}) collective-permute-start(f32[2,64,256]{2,1,0:T(8,128)S(1)} %get-tuple-element.30), channel_id=1, source_target_pairs={{0,1},{1,2},{2,3},{4,5},{5,6},{6,7},{8,9},{9,10},{10,11},{12,13},{... | collective-permute-start | bytes 393224 | tf_op jit(solution)/shard_map/ppermute | solution.py:441
  25.1 4.2 %collective-permute-start.8 = (f32[2,64,256]{2,1,0:T(8,128)S(1)}, f32[2,64,256]{2,1,0:T(8,128)S(1)}, u32[]{:S(2)}, u32[]{:S(2)}) collective-permute-start(f32[2,64,256]{2,1,0:T(8,128)S(1)} %get-tuple-element.31), channel_id=1, source_target_pairs={{0,4},{4,8},{8,12},{12,16},{16,20},{20,24},{24,28},{1,5},{5,9},{9,... | collective-permute-start | bytes 393224 | tf_op jit(solution)/shard_map/ppermute | solution.py:441
  29.3 1.6 %collective-permute-start.2 = (f32[32,128]{1,0:T(8,128)S(1)}, f32[32,128]{1,0:T(8,128)S(1)}, u32[]{:S(2)}, u32[]{:S(2)}) collective-permute-start(f32[32,128]{1,0:T(8,128)S(1)} %get-tuple-element.25), channel_id=1, source_target_pairs={{0,1},{1,0},{2,3},{3,2},{4,5},{5,4},{6,7},{7,6},{8,9},{9,8},{10,11... | collective-permute-start | bytes 49160 | tf_op jit(solution)/shard_map/ppermute | solution.py:402
  30.9 0.8 %collective-permute-done.2 = f32[32,128]{1,0:T(8,128)S(1)} collective-permute-done((f32[32,128]{1,0:T(8,128)S(1)}, f32[32,128]{1,0:T(8,128)S(1)}, u32[]{:S(2)}, u32[]{:S(2)}) %collective-permute-start.2) | collective-permute-done | bytes 16416 | tf_op jit(solution)/shard_map/ppermute | solution.py:402
  31.8 0.5 %collective-permute-start.3 = (f32[32,128]{1,0:T(8,128)S(1)}, f32[32,128]{1,0:T(8,128)S(1)}, u32[]{:S(2)}, u32[]{:S(2)}) collective-permute-start(f32[32,128]{1,0:T(8,128)S(1)} %add.15), channel_id=1, source_target_pairs={{0,2},{1,3},{2,0},{3,1},{4,6},{5,7},{6,4},{7,5},{8,10},{9,11},{10,... | collective-permute-start | bytes 49160 | tf_op jit(solution)/shard_map/ppermute | solution.py:402
  32.3 3.2 %collective-permute-done.3 = f32[32,128]{1,0:T(8,128)S(1)} collective-permute-done((f32[32,128]{1,0:T(8,128)S(1)}, f32[32,128]{1,0:T(8,128)S(1)}, u32[]{:S(2)}, u32[]{:S(2)}) %collective-permute-start.3) | collective-permute-done | bytes 16416 | tf_op jit(solution)/shard_map/ppermute | solution.py:402
  35.5 0.6 %collective-permute-start.4 = (f32[32,128]{1,0:T(8,128)S(1)}, f32[32,128]{1,0:T(8,128)S(1)}, u32[]{:S(2)}, u32[]{:S(2)}) collective-permute-start(f32[32,128]{1,0:T(8,128)S(1)} %add.16), channel_id=1, source_target_pairs={{0,4},{4,0},{8,12},{12,8},{16,20},{20,16},{24,28},{28,24},{1,5},{5... | collective-permute-start | bytes 49160 | tf_op jit(solution)/shard_map/ppermute | solution.py:402
  36.1 3.1 %collective-permute-done.4 = f32[32,128]{1,0:T(8,128)S(1)} collective-permute-done((f32[32,128]{1,0:T(8,128)S(1)}, f32[32,128]{1,0:T(8,128)S(1)}, u32[]{:S(2)}, u32[]{:S(2)}) %collective-permute-start.4) | collective-permute-done | bytes 16416 | tf_op jit(solution)/shard_map/ppermute | solution.py:402
  39.3 1.6 %collective-permute-start.5 = (f32[32,128]{1,0:T(8,128)S(1)}, f32[32,128]{1,0:T(8,128)S(1)}, u32[]{:S(2)}, u32[]{:S(2)}) collective-permute-start(f32[32,128]{1,0:T(8,128)S(1)} %add.17), channel_id=1, source_target_pairs={{0,8},{4,12},{8,0},{12,4},{16,24},{20,28},{24,16},{28,20},{1,9},{5... | collective-permute-start | bytes 49160 | tf_op jit(solution)/shard_map/ppermute | solution.py:402
  40.8 2.2 %collective-permute-done.5 = f32[32,128]{1,0:T(8,128)S(1)} collective-permute-done((f32[32,128]{1,0:T(8,128)S(1)}, f32[32,128]{1,0:T(8,128)S(1)}, u32[]{:S(2)}, u32[]{:S(2)}) %collective-permute-start.5) | collective-permute-done | bytes 16416 | tf_op jit(solution)/shard_map/ppermute | solution.py:402
  43.0 2.6 %collective-permute-start.6 = (f32[32,128]{1,0:T(8,128)S(1)}, f32[32,128]{1,0:T(8,128)S(1)}, u32[]{:S(2)}, u32[]{:S(2)}) collective-permute-start(f32[32,128]{1,0:T(8,128)S(1)} %add.18), channel_id=1, source_target_pairs={{0,16},{4,20},{8,24},{12,28},{16,0},{20,4},{24,8},{28,12},{1,17},{... | collective-permute-start | bytes 49160 | tf_op jit(solution)/shard_map/ppermute | solution.py:402
  45.6 2.1 %collective-permute-done.6 = f32[32,128]{1,0:T(8,128)S(1)} collective-permute-done((f32[32,128]{1,0:T(8,128)S(1)}, f32[32,128]{1,0:T(8,128)S(1)}, u32[]{:S(2)}, u32[]{:S(2)}) %collective-permute-start.6) | collective-permute-done | bytes 16416 | tf_op jit(solution)/shard_map/ppermute | solution.py:402
  47.6 0.0 collective-permute-done.7.back_sub_ref
  47.6 0.0 collective-permute-done.8.back_slab_ref
  47.7 4.0 %shard_map.98 = (f32[2,6,2,16,128]{4,3,2,1,0:T(8,128)}, f32[4,5,16,16]{3,2,1,0:T(8,128)}) custom-call(f32[32,128]{1,0:T(8,128)S(1)} %add.19.gram_ref, bf16[4,80,256]{2,1,0:T(8,128)(2,1)S(1)} %get-tuple-element.26.inner_high, bf16[4,80,256]{2,1,0:T(8,128)(2,1)S(1)} %get-tuple-element.27.inner_low, bf16[4,80,256]{2,1,0:T(8,128)(2,1)S(1)} %get-tuple-element.28.rows_high, ...), custom_call_target="tpu_custom_call" | custom-call | flops 2000000000 | bytes 4000000 | tf_op jit(solution)/shard_map/pallas_call | solution.py:499
  (13 shorter events, 0.0 us)
Async XLA Ops:
  0.6 9.5 %copy-start = (f32[2,6,2,16,128]{4,3,2,1,0:T(8,128)S(1)}, f32[2,6,2,16,128]{4,3,2,1,0:T(8,128)}, u32[]{:S(2)}) copy-start(f32[2,6,2,16,128]{4,3,2,1,0:T(8,128)} %start_ref.7) | copy-start | bytes 589828
  0.6 9.5 %copy-start.4 = (s32[2,6]{1,0:T(2,128)S(1)}, s32[2,6]{1,0:T(2,128)}, u32[]{:S(2)}) copy-start(s32[2,6]{1,0:T(2,128)} %partner_ref.3) | copy-start | bytes 148
  0.7 9.5 %copy-start.1 = (s32[2,16]{1,0:T(2,128)S(1)}, s32[2,16]{1,0:T(2,128)}, u32[]{:S(2)}) copy-start(s32[2,16]{1,0:T(2,128)} %face_ref.1) | copy-start | bytes 388
  0.7 9.5 %copy-start.2 = (s32[2,16]{1,0:T(2,128)S(1)}, s32[2,16]{1,0:T(2,128)}, u32[]{:S(2)}) copy-start(s32[2,16]{1,0:T(2,128)} %class_ref.1) | copy-start | bytes 388
  0.7 9.5 %copy-start.3 = (s32[2,6]{1,0:T(2,128)S(1)}, s32[2,6]{1,0:T(2,128)}, u32[]{:S(2)}) copy-start(s32[2,6]{1,0:T(2,128)} %partner_face_ref.1) | copy-start | bytes 148
  7.6 6.2 %collective-permute-start = (f32[2,160,256]{2,1,0:T(8,128)S(1)}, f32[2,160,256]{2,1,0:T(8,128)S(1)}, u32[]{:S(2)}, u32[]{:S(2)}) collective-permute-start(f32[2,160,256]{2,1,0:T(8,128)S(1)} %get-tuple-element.22), channel_id=1, source_target_pairs={{1,0},{2,1},{3,2},{5,4},{6,5},{7,6},{9,8},{10,9},{11,10},{13,12},{... | collective-permute-start | bytes 983048 | tf_op jit(solution)/shard_map/ppermute | solution.py:441
  8.9 12.3 %collective-permute-start.1 = (f32[2,160,256]{2,1,0:T(8,128)S(1)}, f32[2,160,256]{2,1,0:T(8,128)S(1)}, u32[]{:S(2)}, u32[]{:S(2)}) collective-permute-start(f32[2,160,256]{2,1,0:T(8,128)S(1)} %get-tuple-element.23), channel_id=1, source_target_pairs={{4,0},{8,4},{12,8},{16,12},{20,16},{24,20},{28,24},{5,1},{9,5},{13... | collective-permute-start | bytes 983048 | tf_op jit(solution)/shard_map/ppermute | solution.py:441
  23.1 24.6 %collective-permute-start.7 = (f32[2,64,256]{2,1,0:T(8,128)S(1)}, f32[2,64,256]{2,1,0:T(8,128)S(1)}, u32[]{:S(2)}, u32[]{:S(2)}) collective-permute-start(f32[2,64,256]{2,1,0:T(8,128)S(1)} %get-tuple-element.30), channel_id=1, source_target_pairs={{0,1},{1,2},{2,3},{4,5},{5,6},{6,7},{8,9},{9,10},{10,11},{12,13},{... | collective-permute-start | bytes 393224 | tf_op jit(solution)/shard_map/ppermute | solution.py:441
  25.1 22.5 %collective-permute-start.8 = (f32[2,64,256]{2,1,0:T(8,128)S(1)}, f32[2,64,256]{2,1,0:T(8,128)S(1)}, u32[]{:S(2)}, u32[]{:S(2)}) collective-permute-start(f32[2,64,256]{2,1,0:T(8,128)S(1)} %get-tuple-element.31), channel_id=1, source_target_pairs={{0,4},{4,8},{8,12},{12,16},{16,20},{20,24},{24,28},{1,5},{5,9},{9,... | collective-permute-start | bytes 393224 | tf_op jit(solution)/shard_map/ppermute | solution.py:441
  29.3 2.5 %collective-permute-start.2 = (f32[32,128]{1,0:T(8,128)S(1)}, f32[32,128]{1,0:T(8,128)S(1)}, u32[]{:S(2)}, u32[]{:S(2)}) collective-permute-start(f32[32,128]{1,0:T(8,128)S(1)} %get-tuple-element.25), channel_id=1, source_target_pairs={{0,1},{1,0},{2,3},{3,2},{4,5},{5,4},{6,7},{7,6},{8,9},{9,8},{10,11... | collective-permute-start | bytes 49160 | tf_op jit(solution)/shard_map/ppermute | solution.py:402
  31.8 3.7 %collective-permute-start.3 = (f32[32,128]{1,0:T(8,128)S(1)}, f32[32,128]{1,0:T(8,128)S(1)}, u32[]{:S(2)}, u32[]{:S(2)}) collective-permute-start(f32[32,128]{1,0:T(8,128)S(1)} %add.15), channel_id=1, source_target_pairs={{0,2},{1,3},{2,0},{3,1},{4,6},{5,7},{6,4},{7,5},{8,10},{9,11},{10,... | collective-permute-start | bytes 49160 | tf_op jit(solution)/shard_map/ppermute | solution.py:402
  35.5 3.7 %collective-permute-start.4 = (f32[32,128]{1,0:T(8,128)S(1)}, f32[32,128]{1,0:T(8,128)S(1)}, u32[]{:S(2)}, u32[]{:S(2)}) collective-permute-start(f32[32,128]{1,0:T(8,128)S(1)} %add.16), channel_id=1, source_target_pairs={{0,4},{4,0},{8,12},{12,8},{16,20},{20,16},{24,28},{28,24},{1,5},{5... | collective-permute-start | bytes 49160 | tf_op jit(solution)/shard_map/ppermute | solution.py:402
  39.3 3.7 %collective-permute-start.5 = (f32[32,128]{1,0:T(8,128)S(1)}, f32[32,128]{1,0:T(8,128)S(1)}, u32[]{:S(2)}, u32[]{:S(2)}) collective-permute-start(f32[32,128]{1,0:T(8,128)S(1)} %add.17), channel_id=1, source_target_pairs={{0,8},{4,12},{8,0},{12,4},{16,24},{20,28},{24,16},{28,20},{1,9},{5... | collective-permute-start | bytes 49160 | tf_op jit(solution)/shard_map/ppermute | solution.py:402
  43.0 4.6 %collective-permute-start.6 = (f32[32,128]{1,0:T(8,128)S(1)}, f32[32,128]{1,0:T(8,128)S(1)}, u32[]{:S(2)}, u32[]{:S(2)}) collective-permute-start(f32[32,128]{1,0:T(8,128)S(1)} %add.18), channel_id=1, source_target_pairs={{0,16},{4,20},{8,24},{12,28},{16,0},{20,4},{24,8},{28,12},{1,17},{... | collective-permute-start | bytes 49160 | tf_op jit(solution)/shard_map/ppermute | solution.py:402
